TPU v7x, 128 devices: a whole 4x4x4 slice. The times are simulated.
128 devices in a mesh: sec: 2 (over core), tile: 64 (over z, y, x).
Axes of the slice: x: 4, y: 4, z: 4, core: 2. Of those that a mesh axis runs over, the one named last changes fastest.
Arguments:
- adjoint_state: bfloat16 [2, 75, 2359296], P('sec', None, 'tile'), may hold values from -6 to 6
- tangent_coef: bfloat16 [2, 75, 2359296], P('sec', None, 'tile'), may hold values from 0.5 to 1.5
- column_ops: bfloat16 [2, 16, 75, 75], P('sec')
- surf_read: bfloat16 [2, 4, 75], P('sec'), may hold values from -0.75 to 0.75
- surf_write: float32 [2, 75, 4], P('sec'), may hold values from -3 to 3
- remap_weights: bfloat16 [64, 64, 16, 4096], P('tile')
- pair_atmos: int32 [64, 64, 16], P('tile'), may hold values from 0 to 575
- pair_ocean: int32 [64, 64, 16], P('tile'), may hold values from 0 to 36863, as said below
- list_len: int32 [64, 64], P('tile'), may hold values from 0 to 16, as said below
- ocean_owned: int32 [64, 576], P('tile'), may hold values from 0 to 36863, as said below
Outputs:
- adjoint_out: bfloat16 [2, 75, 2359296], P('sec', None, 'tile')
Inputs may be any that keep to these rules, and one draw needn't show every extreme that they name: pair_ocean[t, d, c] is one of the blocks in row d of ocean_owned. Every global ocean block stands exactly once in ocean_owned. Slots c >= list_len[t, d] are empty; in every draw some ocean tile receives a full list of 16 pairs from every atmosphere tile.
All inputs are finite; a program needn't handle non-finite values.
Results may differ from a plain program's by a relative error of at most 0.012.
Values may be sent and summed in bfloat16 or wider, within the bound.
No kernel may reach another device: no remote copies, remote signals or barrier semaphores. Data moves between devices by JAX's collectives and lax.ppermute only.
A program may use at most 128 MiB of HBM per device.

v0:
```python
import jax
import jax.numpy as jnp
from jax import lax
from jax.sharding import PartitionSpec as P

NF = 4
BLK = 64
NSTEP = 16


def shifted(value, axis, steps):
    count = lax.axis_size(axis)
    first, last = (max(0, -steps), min(count, count - steps))
    return lax.ppermute(value, axis, [(source, source + steps) for source in range(first, last)])


def locate_blocks(arrived_ids, owned_row, slot_count, blocks):
    matches = arrived_ids.reshape(slot_count)[:, None] == owned_row[None, :]
    return jnp.sum(
        jnp.where(matches, lax.broadcasted_iota(jnp.int32, (slot_count, blocks), 1), 0), axis=1
    )


def forward_remap(picked, paired_weights, slot_count):
    half = BLK // 2
    split_rows = picked.reshape(slot_count, NF, half, 2)
    even_rows = split_rows[:, :, :, 0]
    odd_rows = split_rows[:, :, :, 1]
    first = jnp.einsum(
        "snj,sjq->snq", even_rows, paired_weights, preferred_element_type=jnp.float32
    )
    second = jnp.einsum(
        "snj,sjq->snq", odd_rows, paired_weights, preferred_element_type=jnp.float32
    )
    return first[:, :, :BLK] + second[:, :, BLK:]


def backward_remap(echoes, paired_weights, slot_count):
    blank = jnp.zeros_like(echoes)
    lower = jnp.concatenate([echoes, blank], 2)
    upper = jnp.concatenate([blank, echoes], 2)
    even_cells = jnp.einsum(
        "sjq,snq->snj", paired_weights, lower, preferred_element_type=jnp.float32
    )
    odd_cells = jnp.einsum(
        "sjq,snq->snj", paired_weights, upper, preferred_element_type=jnp.float32
    )
    return jnp.stack([even_cells, odd_cells], 3).reshape(slot_count, NF, BLK)


def body(
    adjoint_state,
    tangent_coef,
    column_ops,
    surf_read,
    surf_write,
    remap_weights,
    pair_atmos,
    pair_ocean,
    list_len,
    ocean_owned,
):
    tile_count = lax.axis_size("tile")
    section = lax.axis_index("sec")
    slot_cap = pair_atmos.shape[2]
    slot_count = tile_count * slot_cap
    blocks = ocean_owned.shape[1]
    column = adjoint_state[0]
    surface = jnp.dot(surf_read[0], column, preferred_element_type=jnp.float32).astype(jnp.bfloat16)
    surface_blocks = surface.reshape(NF, blocks, BLK).transpose(1, 0, 2)
    ocean_rows = surface_blocks.reshape(blocks, NF * BLK)
    paired_weights = remap_weights[0].reshape(slot_count, BLK // 2, 2 * BLK)
    source = pair_atmos[0].reshape(slot_count)
    live_mask = (
        lax.broadcasted_iota(jnp.int32, (tile_count, slot_cap), 1) < list_len[0][:, None]
    ).reshape(slot_count, 1, 1)
    picked = surface_blocks[source]
    partial_flux = forward_remap(picked, paired_weights, slot_count)
    partial_flux = jnp.where(live_mask, partial_flux, 0.0).reshape(tile_count, slot_cap, NF * BLK)
    targets = pair_ocean[0]
    received, arrived_ids = (
        lax.all_to_all(partial_flux, "tile", split_axis=0, concat_axis=0, tiled=True),
        lax.all_to_all(targets, "tile", split_axis=0, concat_axis=0, tiled=True),
    )
    arriving = shifted(received, "sec", 1)
    position = locate_blocks(arrived_ids, ocean_owned[0], slot_count, blocks)
    replies = ocean_rows[position].reshape(tile_count, slot_cap, NF * BLK)
    crossed = shifted(replies, "sec", -1)
    returned = lax.all_to_all(crossed, "tile", split_axis=0, concat_axis=0, tiled=True)
    ocean_terms = jax.ops.segment_sum(
        arriving.reshape(slot_count, NF * BLK), position, num_segments=blocks
    )
    ocean_forcing = (
        ocean_terms.reshape(blocks, NF, BLK).transpose(1, 0, 2).reshape(NF, blocks * BLK)
    )
    echoes = returned.reshape(slot_count, NF, BLK)
    back_terms = backward_remap(echoes, paired_weights, slot_count)
    back_terms = jnp.where(live_mask, back_terms, 0.0).reshape(slot_count, NF * BLK)
    atmos_terms = jax.ops.segment_sum(back_terms, source, num_segments=blocks)
    atmos_forcing = (
        atmos_terms.reshape(blocks, NF, BLK).transpose(1, 0, 2).reshape(NF, blocks * BLK)
    )
    forcing = jnp.where(section == 0, atmos_forcing, ocean_forcing)
    factors = tangent_coef[0]

    def advance(step_index, current):
        operator = column_ops[0, step_index]
        stepped = lax.dot_general(
            operator, current, (((0,), (0,)), ((), ())), preferred_element_type=jnp.float32
        )
        return (stepped * factors).astype(jnp.bfloat16)

    swept_state = lax.fori_loop(0, NSTEP, advance, column)
    result = swept_state.astype(jnp.float32) + jnp.dot(
        surf_write[0], forcing, precision=lax.Precision.HIGHEST
    )
    return result.astype(jnp.bfloat16)[None]


def solution(mesh):
    in_specs = (
        P("sec", None, "tile"),
        P("sec", None, "tile"),
        P("sec", None, None, None),
        P("sec", None, None),
        P("sec", None, None),
        P("tile", None, None, None),
        P("tile", None, None),
        P("tile", None, None),
        P("tile", None),
        P("tile", None),
    )
    out_specs = P("sec", None, "tile")
    return jax.shard_map(body, mesh=mesh, in_specs=in_specs, out_specs=out_specs, check_vma=False)
```

profile of v0, /device:TPU:1, one launch (start us, length us, event | category | flops | bytes accessed | tf_op | source)
XLA Modules:
  0.0 272.2 jit_solution(3038483180853067617)
XLA Ops:
  0.0 5.7 %copy.81 = bf16[1,75,36864]{2,1,0:T(8,128)(2,1)} copy(bf16[1,75,36864]{2,1,0:T(8,128)(2,1)} %param.12) | data formatting | bytes 11059200
  6.4 12.0 %all-to-all-start = ((s32[64,1,16]{2,1,0:T(1,128)}), s32[64,1,16]{2,1,0:T(1,128)S(1)}, u32[]{:S(2)}, u32[]{:S(2)}) async-start(s32[64,1,16]{2,1,0:T(1,128)} %bitcast.7), calls=%async_computation | async-start | bytes 65536 | tf_op jit(solution)/shard_map/all_to_all | solution.py:83
  18.3 9.6 %copy.71 = bf16[128,8,32,128]{3,2,1,0:T(8,128)(2,1)} copy(bf16[128,8,32,128]{3,1,2,0:T(8,128)(2,1)} %bitcast.70) | data formatting | bytes 16777216
  30.0 3.6 %gather_fusion.1 = bf16[1024,4,64]{2,1,0:T(4,128)(2,1)S(1)} fusion(bf16[576,4,64]{2,1,0:T(4,128)(2,1)S(1)} %bitcast.68, s32[1024]{0:T(1024)S(1)} %broadcast_clamp_fusion), kind=kCustom, calls=%fused_computation.1 | custom fusion | bytes 1052672 | tf_op jit(solution)/shard_map/gather | solution.py:77
  37.0 6.0 %fusion.7 = f32[1024,4,64]{2,1,0:T(4,128)S(1)} fusion(bf16[1024,32,128]{2,1,0:T(8,128)(2,1)} %bitcast.64, bf16[1024,4,32,1]{2,1,0,3:T(4,128)(2,1)S(1)} %copy.70), kind=kOutput, calls=%fused_computation.14 | convolution fusion | flops 16777216 | bytes 9699328 | tf_op jit(solution)/shard_map/snj,sjq->snq/dot_general | solution.py:32
  43.0 6.0 %add_select_fusion = f32[1024,4,64]{2,1,0:T(4,128)S(1)} fusion(f32[1024,4,64]{2,1,0:T(4,128)S(1)} %fusion.7, bf16[1024,32,128]{2,1,0:T(8,128)(2,1)} %bitcast.65, bf16[1024,4,32,1]{2,1,0,3:T(4,128)(2,1)S(1)} %copy-done.4, pred[1024]{0:T(1024)(128)(4,1)S(1)} %lt.50), kind=kOutput, calls=%fused_computation.20 | convolution fusion | flops 17301504 | bytes 10748928 | tf_op jit(solution)/shard_map/snj,sjq->snq/dot_general | solution.py:29
  49.5 2.2 reshape.101
  51.9 10.0 %all-to-all-start.2 = ((f32[64,16,256]{2,1,0:T(8,128)}), f32[64,16,256]{2,1,0:T(8,128)S(1)}, u32[]{:S(2)}, u32[]{:S(2)}) async-start(f32[64,16,256]{2,1,0:T(8,128)} %reshape.101), calls=%async_computation.2 | async-start | bytes 2097152 | tf_op jit(solution)/shard_map/all_to_all | solution.py:82
  63.7 3.9 %gather_fusion = bf16[1024,256]{1,0:T(8,128)(2,1)S(1)} fusion(bf16[576,256]{1,0:T(8,128)(2,1)S(1)} %copy.60, s32[1024]{0:T(1024)S(1)} %broadcast_clamp_fusion.1), kind=kCustom, calls=%fused_computation | custom fusion | bytes 1052672 | tf_op jit(solution)/shard_map/gather | solution.py:87
  67.6 4.2 %collective-permute-start = (bf16[64,16,256]{2,1,0:T(8,128)(2,1)S(1)}, bf16[64,16,256]{2,1,0:T(8,128)(2,1)}, u32[]{:S(2)}, u32[]{:S(2)}) collective-permute-start(bf16[64,16,256]{2,1,0:T(8,128)(2,1)S(1)} %bitcast.74), channel_id=1, source_target_pairs={{64,0},{65,1},{66,2},{67,3},{68,4},{69,5},{70,6},{71,7},{72,8},{73... | collective-permute-start | bytes 1572872 | tf_op jit(solution)/shard_map/ppermute | solution.py:14
  72.7 6.3 %all-to-all-done.2 = f32[64,16,256]{2,1,0:T(8,128)S(1)} async-done(((f32[64,16,256]{2,1,0:T(8,128)}), f32[64,16,256]{2,1,0:T(8,128)S(1)}, u32[]{:S(2)}, u32[]{:S(2)}) %all-to-all-start.2) | async-done | bytes 1048608 | tf_op jit(solution)/shard_map/all_to_all | solution.py:82
  79.0 4.7 %all-to-all-start.1 = ((bf16[64,16,256]{2,1,0:T(8,128)(2,1)}), bf16[64,16,256]{2,1,0:T(8,128)(2,1)S(1)}, u32[]{:S(2)}, u32[]{:S(2)}) async-start(bf16[64,16,256]{2,1,0:T(8,128)(2,1)} %collective-permute-done), calls=%async_computation.1 | async-start | bytes 1048576 | tf_op jit(solution)/shard_map/all_to_all | solution.py:89
  83.7 139.1 %while.13 = (s32[]{:T(128)}, bf16[75,36864]{1,0:T(8,128)(2,1)}, bf16[1,16,75,75]{3,2,1,0:T(8,128)(2,1)S(1)}, bf16[75,36864]{1,0:T(8,128)(2,1)}, s32[]{:T(128)}) while((s32[]{:T(128)}, bf16[75,36864]{1,0:T(8,128)(2,1)}, bf16[1,16,75,75]{3,2,1,0:T(8,128)(2,1)S(1)}, bf16[75,36864]{1,0:T(8,128)(2,1)}, s32[]{:T(128)}) %tuple.37), condition=%wide.region_1.2_spmd, body=%wide.region_0.1_spmd.sunk | while | flops 423014400 | bytes 50524252 | solution.py:113
  83.7 2.8 %copy.82 = bf16[75,36864]{1,0:T(8,128)(2,1)S(1)} copy(bf16[75,36864]{1,0:T(8,128)(2,1)} %get-tuple-element.142) | data formatting | bytes 11059200 | tf_op jit(solution)/shard_map/while
  88.1 4.3 %fusion.36 = bf16[75,36864]{1,0:T(8,128)(2,1)} fusion(bf16[75,36864]{1,0:T(8,128)(2,1)S(1)} %copy.82, bf16[75,36864]{1,0:T(8,128)(2,1)S(1)} %copy-done.2, bf16[1,16,75,75]{3,2,1,0:T(8,128)(2,1)S(1)} %get-tuple-element.148, s32[]{:T(128)} %get-tuple-element.141), kind=kOutput, calls=%fused_computation.5.clone.1 | convolution fusion | flops 423014400 | bytes 17346564 | tf_op jit(solution)/shard_map/while/body/eval_jaxpr/dot_general | solution.py:108
  92.4 2.8 %copy.82 = bf16[75,36864]{1,0:T(8,128)(2,1)S(1)} copy(bf16[75,36864]{1,0:T(8,128)(2,1)} %get-tuple-element.142) | data formatting | bytes 11059200 | tf_op jit(solution)/shard_map/while
  95.2 1.6 copy-done.2
  96.8 4.3 %fusion.36 = bf16[75,36864]{1,0:T(8,128)(2,1)} fusion(bf16[75,36864]{1,0:T(8,128)(2,1)S(1)} %copy.82, bf16[75,36864]{1,0:T(8,128)(2,1)S(1)} %copy-done.2, bf16[1,16,75,75]{3,2,1,0:T(8,128)(2,1)S(1)} %get-tuple-element.148, s32[]{:T(128)} %get-tuple-element.141), kind=kOutput, calls=%fused_computation.5.clone.1 | convolution fusion | flops 423014400 | bytes 17346564 | tf_op jit(solution)/shard_map/while/body/eval_jaxpr/dot_general | solution.py:108
  101.1 2.8 %copy.82 = bf16[75,36864]{1,0:T(8,128)(2,1)S(1)} copy(bf16[75,36864]{1,0:T(8,128)(2,1)} %get-tuple-element.142) | data formatting | bytes 11059200 | tf_op jit(solution)/shard_map/while
  103.9 1.6 copy-done.2
  105.5 4.3 %fusion.36 = bf16[75,36864]{1,0:T(8,128)(2,1)} fusion(bf16[75,36864]{1,0:T(8,128)(2,1)S(1)} %copy.82, bf16[75,36864]{1,0:T(8,128)(2,1)S(1)} %copy-done.2, bf16[1,16,75,75]{3,2,1,0:T(8,128)(2,1)S(1)} %get-tuple-element.148, s32[]{:T(128)} %get-tuple-element.141), kind=kOutput, calls=%fused_computation.5.clone.1 | convolution fusion | flops 423014400 | bytes 17346564 | tf_op jit(solution)/shard_map/while/body/eval_jaxpr/dot_general | solution.py:108
  109.8 2.8 %copy.82 = bf16[75,36864]{1,0:T(8,128)(2,1)S(1)} copy(bf16[75,36864]{1,0:T(8,128)(2,1)} %get-tuple-element.142) | data formatting | bytes 11059200 | tf_op jit(solution)/shard_map/while
  112.6 1.6 copy-done.2
  114.2 4.3 %fusion.36 = bf16[75,36864]{1,0:T(8,128)(2,1)} fusion(bf16[75,36864]{1,0:T(8,128)(2,1)S(1)} %copy.82, bf16[75,36864]{1,0:T(8,128)(2,1)S(1)} %copy-done.2, bf16[1,16,75,75]{3,2,1,0:T(8,128)(2,1)S(1)} %get-tuple-element.148, s32[]{:T(128)} %get-tuple-element.141), kind=kOutput, calls=%fused_computation.5.clone.1 | convolution fusion | flops 423014400 | bytes 17346564 | tf_op jit(solution)/shard_map/while/body/eval_jaxpr/dot_general | solution.py:108
  118.5 2.8 %copy.82 = bf16[75,36864]{1,0:T(8,128)(2,1)S(1)} copy(bf16[75,36864]{1,0:T(8,128)(2,1)} %get-tuple-element.142) | data formatting | bytes 11059200 | tf_op jit(solution)/shard_map/while
  121.3 1.6 copy-done.2
  122.9 4.3 %fusion.36 = bf16[75,36864]{1,0:T(8,128)(2,1)} fusion(bf16[75,36864]{1,0:T(8,128)(2,1)S(1)} %copy.82, bf16[75,36864]{1,0:T(8,128)(2,1)S(1)} %copy-done.2, bf16[1,16,75,75]{3,2,1,0:T(8,128)(2,1)S(1)} %get-tuple-element.148, s32[]{:T(128)} %get-tuple-element.141), kind=kOutput, calls=%fused_computation.5.clone.1 | convolution fusion | flops 423014400 | bytes 17346564 | tf_op jit(solution)/shard_map/while/body/eval_jaxpr/dot_general | solution.py:108
  127.2 2.8 %copy.82 = bf16[75,36864]{1,0:T(8,128)(2,1)S(1)} copy(bf16[75,36864]{1,0:T(8,128)(2,1)} %get-tuple-element.142) | data formatting | bytes 11059200 | tf_op jit(solution)/shard_map/while
  130.0 1.6 copy-done.2
  131.6 4.3 %fusion.36 = bf16[75,36864]{1,0:T(8,128)(2,1)} fusion(bf16[75,36864]{1,0:T(8,128)(2,1)S(1)} %copy.82, bf16[75,36864]{1,0:T(8,128)(2,1)S(1)} %copy-done.2, bf16[1,16,75,75]{3,2,1,0:T(8,128)(2,1)S(1)} %get-tuple-element.148, s32[]{:T(128)} %get-tuple-element.141), kind=kOutput, calls=%fused_computation.5.clone.1 | convolution fusion | flops 423014400 | bytes 17346564 | tf_op jit(solution)/shard_map/while/body/eval_jaxpr/dot_general | solution.py:108
  135.9 2.8 %copy.82 = bf16[75,36864]{1,0:T(8,128)(2,1)S(1)} copy(bf16[75,36864]{1,0:T(8,128)(2,1)} %get-tuple-element.142) | data formatting | bytes 11059200 | tf_op jit(solution)/shard_map/while
  138.7 1.6 copy-done.2
  140.3 4.3 %fusion.36 = bf16[75,36864]{1,0:T(8,128)(2,1)} fusion(bf16[75,36864]{1,0:T(8,128)(2,1)S(1)} %copy.82, bf16[75,36864]{1,0:T(8,128)(2,1)S(1)} %copy-done.2, bf16[1,16,75,75]{3,2,1,0:T(8,128)(2,1)S(1)} %get-tuple-element.148, s32[]{:T(128)} %get-tuple-element.141), kind=kOutput, calls=%fused_computation.5.clone.1 | convolution fusion | flops 423014400 | bytes 17346564 | tf_op jit(solution)/shard_map/while/body/eval_jaxpr/dot_general | solution.py:108
  144.6 2.8 %copy.82 = bf16[75,36864]{1,0:T(8,128)(2,1)S(1)} copy(bf16[75,36864]{1,0:T(8,128)(2,1)} %get-tuple-element.142) | data formatting | bytes 11059200 | tf_op jit(solution)/shard_map/while
  147.4 1.6 copy-done.2
  149.0 4.3 %fusion.36 = bf16[75,36864]{1,0:T(8,128)(2,1)} fusion(bf16[75,36864]{1,0:T(8,128)(2,1)S(1)} %copy.82, bf16[75,36864]{1,0:T(8,128)(2,1)S(1)} %copy-done.2, bf16[1,16,75,75]{3,2,1,0:T(8,128)(2,1)S(1)} %get-tuple-element.148, s32[]{:T(128)} %get-tuple-element.141), kind=kOutput, calls=%fused_computation.5.clone.1 | convolution fusion | flops 423014400 | bytes 17346564 | tf_op jit(solution)/shard_map/while/body/eval_jaxpr/dot_general | solution.py:108
  153.3 2.8 %copy.82 = bf16[75,36864]{1,0:T(8,128)(2,1)S(1)} copy(bf16[75,36864]{1,0:T(8,128)(2,1)} %get-tuple-element.142) | data formatting | bytes 11059200 | tf_op jit(solution)/shard_map/while
  156.1 1.6 copy-done.2
  157.6 4.3 %fusion.36 = bf16[75,36864]{1,0:T(8,128)(2,1)} fusion(bf16[75,36864]{1,0:T(8,128)(2,1)S(1)} %copy.82, bf16[75,36864]{1,0:T(8,128)(2,1)S(1)} %copy-done.2, bf16[1,16,75,75]{3,2,1,0:T(8,128)(2,1)S(1)} %get-tuple-element.148, s32[]{:T(128)} %get-tuple-element.141), kind=kOutput, calls=%fused_computation.5.clone.1 | convolution fusion | flops 423014400 | bytes 17346564 | tf_op jit(solution)/shard_map/while/body/eval_jaxpr/dot_general | solution.py:108
  161.9 2.8 %copy.82 = bf16[75,36864]{1,0:T(8,128)(2,1)S(1)} copy(bf16[75,36864]{1,0:T(8,128)(2,1)} %get-tuple-element.142) | data formatting | bytes 11059200 | tf_op jit(solution)/shard_map/while
  166.3 4.3 %fusion.36 = bf16[75,36864]{1,0:T(8,128)(2,1)} fusion(bf16[75,36864]{1,0:T(8,128)(2,1)S(1)} %copy.82, bf16[75,36864]{1,0:T(8,128)(2,1)S(1)} %copy-done.2, bf16[1,16,75,75]{3,2,1,0:T(8,128)(2,1)S(1)} %get-tuple-element.148, s32[]{:T(128)} %get-tuple-element.141), kind=kOutput, calls=%fused_computation.5.clone.1 | convolution fusion | flops 423014400 | bytes 17346564 | tf_op jit(solution)/shard_map/while/body/eval_jaxpr/dot_general | solution.py:108
  170.6 2.8 %copy.82 = bf16[75,36864]{1,0:T(8,128)(2,1)S(1)} copy(bf16[75,36864]{1,0:T(8,128)(2,1)} %get-tuple-element.142) | data formatting | bytes 11059200 | tf_op jit(solution)/shard_map/while
  173.5 1.6 copy-done.2
  175.0 4.3 %fusion.36 = bf16[75,36864]{1,0:T(8,128)(2,1)} fusion(bf16[75,36864]{1,0:T(8,128)(2,1)S(1)} %copy.82, bf16[75,36864]{1,0:T(8,128)(2,1)S(1)} %copy-done.2, bf16[1,16,75,75]{3,2,1,0:T(8,128)(2,1)S(1)} %get-tuple-element.148, s32[]{:T(128)} %get-tuple-element.141), kind=kOutput, calls=%fused_computation.5.clone.1 | convolution fusion | flops 423014400 | bytes 17346564 | tf_op jit(solution)/shard_map/while/body/eval_jaxpr/dot_general | solution.py:108
  179.3 2.8 %copy.82 = bf16[75,36864]{1,0:T(8,128)(2,1)S(1)} copy(bf16[75,36864]{1,0:T(8,128)(2,1)} %get-tuple-element.142) | data formatting | bytes 11059200 | tf_op jit(solution)/shard_map/while
  182.1 1.6 copy-done.2
  183.7 4.3 %fusion.36 = bf16[75,36864]{1,0:T(8,128)(2,1)} fusion(bf16[75,36864]{1,0:T(8,128)(2,1)S(1)} %copy.82, bf16[75,36864]{1,0:T(8,128)(2,1)S(1)} %copy-done.2, bf16[1,16,75,75]{3,2,1,0:T(8,128)(2,1)S(1)} %get-tuple-element.148, s32[]{:T(128)} %get-tuple-element.141), kind=kOutput, calls=%fused_computation.5.clone.1 | convolution fusion | flops 423014400 | bytes 17346564 | tf_op jit(solution)/shard_map/while/body/eval_jaxpr/dot_general | solution.py:108
  188.0 2.8 %copy.82 = bf16[75,36864]{1,0:T(8,128)(2,1)S(1)} copy(bf16[75,36864]{1,0:T(8,128)(2,1)} %get-tuple-element.142) | data formatting | bytes 11059200 | tf_op jit(solution)/shard_map/while
  192.4 4.3 %fusion.36 = bf16[75,36864]{1,0:T(8,128)(2,1)} fusion(bf16[75,36864]{1,0:T(8,128)(2,1)S(1)} %copy.82, bf16[75,36864]{1,0:T(8,128)(2,1)S(1)} %copy-done.2, bf16[1,16,75,75]{3,2,1,0:T(8,128)(2,1)S(1)} %get-tuple-element.148, s32[]{:T(128)} %get-tuple-element.141), kind=kOutput, calls=%fused_computation.5.clone.1 | convolution fusion | flops 423014400 | bytes 17346564 | tf_op jit(solution)/shard_map/while/body/eval_jaxpr/dot_general | solution.py:108
  196.7 2.8 %copy.82 = bf16[75,36864]{1,0:T(8,128)(2,1)S(1)} copy(bf16[75,36864]{1,0:T(8,128)(2,1)} %get-tuple-element.142) | data formatting | bytes 11059200 | tf_op jit(solution)/shard_map/while
  199.5 1.6 copy-done.2
  201.1 4.3 %fusion.36 = bf16[75,36864]{1,0:T(8,128)(2,1)} fusion(bf16[75,36864]{1,0:T(8,128)(2,1)S(1)} %copy.82, bf16[75,36864]{1,0:T(8,128)(2,1)S(1)} %copy-done.2, bf16[1,16,75,75]{3,2,1,0:T(8,128)(2,1)S(1)} %get-tuple-element.148, s32[]{:T(128)} %get-tuple-element.141), kind=kOutput, calls=%fused_computation.5.clone.1 | convolution fusion | flops 423014400 | bytes 17346564 | tf_op jit(solution)/shard_map/while/body/eval_jaxpr/dot_general | solution.py:108
  205.4 2.8 %copy.82 = bf16[75,36864]{1,0:T(8,128)(2,1)S(1)} copy(bf16[75,36864]{1,0:T(8,128)(2,1)} %get-tuple-element.142) | data formatting | bytes 11059200 | tf_op jit(solution)/shard_map/while
  208.2 1.6 copy-done.2
  209.8 4.3 %fusion.36 = bf16[75,36864]{1,0:T(8,128)(2,1)} fusion(bf16[75,36864]{1,0:T(8,128)(2,1)S(1)} %copy.82, bf16[75,36864]{1,0:T(8,128)(2,1)S(1)} %copy-done.2, bf16[1,16,75,75]{3,2,1,0:T(8,128)(2,1)S(1)} %get-tuple-element.148, s32[]{:T(128)} %get-tuple-element.141), kind=kOutput, calls=%fused_computation.5.clone.1 | convolution fusion | flops 423014400 | bytes 17346564 | tf_op jit(solution)/shard_map/while/body/eval_jaxpr/dot_general | solution.py:108
  214.1 2.8 %copy.82 = bf16[75,36864]{1,0:T(8,128)(2,1)S(1)} copy(bf16[75,36864]{1,0:T(8,128)(2,1)} %get-tuple-element.142) | data formatting | bytes 11059200 | tf_op jit(solution)/shard_map/while
  218.5 4.3 %fusion.36 = bf16[75,36864]{1,0:T(8,128)(2,1)} fusion(bf16[75,36864]{1,0:T(8,128)(2,1)S(1)} %copy.82, bf16[75,36864]{1,0:T(8,128)(2,1)S(1)} %copy-done.2, bf16[1,16,75,75]{3,2,1,0:T(8,128)(2,1)S(1)} %get-tuple-element.148, s32[]{:T(128)} %get-tuple-element.141), kind=kOutput, calls=%fused_computation.5.clone.1 | convolution fusion | flops 423014400 | bytes 17346564 | tf_op jit(solution)/shard_map/while/body/eval_jaxpr/dot_general | solution.py:108
  224.6 8.0 %convolution_bitcast_fusion.1 = f32[1024,4,32,1]{2,1,0,3:T(4,128)S(1)} fusion(bf16[1024,32,128]{2,1,0:T(8,128)(2,1)} %bitcast.66, bf16[1024,4,64]{2,1,0:T(4,128)(2,1)S(1)} %reshape.98), kind=kOutput, calls=%fused_computation.21 | convolution fusion | flops 33554432 | bytes 9437184 | tf_op jit(solution)/shard_map/sjq,snq->snj/dot_general | solution.py:45
  232.6 4.6 %convolution_bitcast_fusion.2 = f32[1024,4,32,1]{2,1,0,3:T(4,128)S(1)} fusion(bf16[1024,32,128]{2,1,0:T(8,128)(2,1)S(1)} %bitcast.67, bf16[1024,4,64]{2,1,0:T(4,128)(2,1)S(1)} %reshape.98), kind=kOutput, calls=%fused_computation.22 | convolution fusion | flops 33554432 | bytes 9437184 | tf_op jit(solution)/shard_map/sjq,snq->snj/dot_general | solution.py:42
  237.2 3.0 %pad_maximum_fusion = f32[1024,4,32,2]{2,1,0,3:T(4,128)} fusion(f32[1024,4,32,1]{2,1,0,3:T(4,128)S(1)} %convolution_bitcast_fusion.1, f32[1024,4,32,1]{2,1,0,3:T(4,128)S(1)} %convolution_bitcast_fusion.2), kind=kLoop, calls=%fused_computation.18 | loop fusion | flops 262144 | bytes 2097152 | tf_op jit(solution)/shard_map/stack | solution.py:48
  240.2 3.6 %copy.61 = f32[1024,4,32,2]{0,3,2,1:T(2,128)S(1)} copy(f32[1024,4,32,2]{2,1,0,3:T(4,128)} %pad_maximum_fusion) | data formatting | bytes 2097152 | tf_op jit(solution)/shard_map/stack | solution.py:48
  245.0 6.4 %scatter_custom_fusion = f32[576,256]{1,0:T(8,128)S(1)} fusion(s32[1024]{0:T(1024)S(1)} %reshape.121, f32[1024,256]{1,0:T(8,128)S(1)} %copy.62, f32[]{:T(128)} %constant.35.clone.1), kind=kCustom, calls=%fused_computation.31 | custom fusion | flops 262144 | bytes 589828 | tf_op jit(solution)/shard_map/scatter-add | solution.py:99
  251.4 6.7 %scatter_custom_fusion.1 = f32[576,256]{1,0:T(8,128)S(1)} fusion(s32[1024]{0:T(1024)S(1)} %select_reduce_fusion, f32[1024,256]{1,0:T(8,128)} %bitcast.17, f32[]{:T(128)} %constant.35.clone.1), kind=kCustom, calls=%fused_computation.29 | custom fusion | flops 262144 | bytes 590336 | tf_op jit(solution)/shard_map/scatter-add | solution.py:90
  259.3 12.9 %fusion.6 = bf16[1,75,36864]{2,1,0:T(8,128)(2,1)} fusion(f32[4,36864]{1,0:T(4,128)S(1)} %select_n.63, bf16[75,36864]{1,0:T(8,128)(2,1)} %get-tuple-element.84, f32[1,75,4]{1,2,0:T(4,128)S(1)} %copy-done), kind=kOutput, calls=%fused_computation.12 | convolution fusion | flops 141004800 | bytes 11650224 | tf_op jit(solution)/shard_map/dot_general | solution.py:114
  (78 shorter events, 19.7 us)
Async XLA Ops:
  0.0 259.3 %copy-start = (f32[1,75,4]{1,2,0:T(4,128)S(1)}, f32[1,75,4]{1,2,0:T(4,128)}, u32[]{:S(2)}) copy-start(f32[1,75,4]{1,2,0:T(4,128)} %param.16) | copy-start | bytes 3604
  0.0 5.7 %copy-start.6 = (s32[1,64,16]{1,2,0:T(8,128)S(1)}, s32[1,64,16]{1,2,0:T(8,128)}, u32[]{:S(2)}) copy-start(s32[1,64,16]{1,2,0:T(8,128)} %param.19) | copy-start | bytes 12292
  6.4 45.5 %all-to-all-start = ((s32[64,1,16]{2,1,0:T(1,128)}), s32[64,1,16]{2,1,0:T(1,128)S(1)}, u32[]{:S(2)}, u32[]{:S(2)}) async-start(s32[64,1,16]{2,1,0:T(1,128)} %bitcast.7), calls=%async_computation | async-start | bytes 65536 | tf_op jit(solution)/shard_map/all_to_all | solution.py:83
  18.3 9.6 %copy-start.1 = (bf16[1,75,36864]{2,1,0:T(8,128)(2,1)S(1)}, bf16[1,75,36864]{2,1,0:T(8,128)(2,1)}, u32[]{:S(2)}) copy-start(bf16[1,75,36864]{2,1,0:T(8,128)(2,1)} %copy.81) | copy-start | bytes 16588804
  18.3 9.6 %copy-start.9 = (bf16[1,4,75]{2,1,0:T(4,128)(2,1)S(1)}, bf16[1,4,75]{2,1,0:T(4,128)(2,1)}, u32[]{:S(2)}) copy-start(bf16[1,4,75]{2,1,0:T(4,128)(2,1)} %param.15) | copy-start | bytes 1804
  27.9 1.8 copy-start.7
  28.8 8.0 %copy-start.10 = (s32[1,64]{1,0:T(1,128)S(1)}, s32[1,64]{1,0:T(1,128)}, u32[]{:S(2)}) copy-start(s32[1,64]{1,0:T(1,128)} %param.20) | copy-start | bytes 772
  37.0 6.0 %copy-start.4 = (bf16[1024,4,32,1]{2,1,0,3:T(4,128)(2,1)S(1)}, bf16[1024,4,32,1]{2,1,0,3:T(4,128)(2,1)}, u32[]{:S(2)}) copy-start(bf16[1024,4,32,1]{2,1,0,3:T(4,128)(2,1)} %copy.69) | copy-start | bytes 786436
  43.0 8.8 %copy-start.8 = (s32[1,576]{1,0:T(1,128)S(1)}, s32[1,576]{1,0:T(1,128)}, u32[]{:S(2)}) copy-start(s32[1,576]{1,0:T(1,128)} %param.21) | copy-start | bytes 6916
  49.1 22.8 %copy-start.5 = (bf16[1,16,75,75]{3,1,2,0:T(8,128)(2,1)S(1)}, bf16[1,16,75,75]{3,1,2,0:T(8,128)(2,1)}, u32[]{:S(2)}) copy-start(bf16[1,16,75,75]{3,1,2,0:T(8,128)(2,1)} %param.14) | copy-start | bytes 540004
  51.9 27.1 %all-to-all-start.2 = ((f32[64,16,256]{2,1,0:T(8,128)}), f32[64,16,256]{2,1,0:T(8,128)S(1)}, u32[]{:S(2)}, u32[]{:S(2)}) async-start(f32[64,16,256]{2,1,0:T(8,128)} %reshape.101), calls=%async_computation.2 | async-start | bytes 2097152 | tf_op jit(solution)/shard_map/all_to_all | solution.py:82
  67.6 5.1 %collective-permute-start = (bf16[64,16,256]{2,1,0:T(8,128)(2,1)S(1)}, bf16[64,16,256]{2,1,0:T(8,128)(2,1)}, u32[]{:S(2)}, u32[]{:S(2)}) collective-permute-start(bf16[64,16,256]{2,1,0:T(8,128)(2,1)S(1)} %bitcast.74), channel_id=1, source_target_pairs={{64,0},{65,1},{66,2},{67,3},{68,4},{69,5},{70,6},{71,7},{72,8},{73... | collective-permute-start | bytes 1572872 | tf_op jit(solution)/shard_map/ppermute | solution.py:14
  79.0 145.1 %all-to-all-start.1 = ((bf16[64,16,256]{2,1,0:T(8,128)(2,1)}), bf16[64,16,256]{2,1,0:T(8,128)(2,1)S(1)}, u32[]{:S(2)}, u32[]{:S(2)}) async-start(bf16[64,16,256]{2,1,0:T(8,128)(2,1)} %collective-permute-done), calls=%async_computation.1 | async-start | bytes 1048576 | tf_op jit(solution)/shard_map/all_to_all | solution.py:89
  83.7 4.4 %copy-start.2 = (bf16[75,36864]{1,0:T(8,128)(2,1)S(1)}, bf16[75,36864]{1,0:T(8,128)(2,1)}, u32[]{:S(2)}) copy-start(bf16[75,36864]{1,0:T(8,128)(2,1)} %get-tuple-element.149) | copy-start | bytes 16588804 | tf_op jit(solution)/shard_map/while
  92.4 4.4 %copy-start.2 = (bf16[75,36864]{1,0:T(8,128)(2,1)S(1)}, bf16[75,36864]{1,0:T(8,128)(2,1)}, u32[]{:S(2)}) copy-start(bf16[75,36864]{1,0:T(8,128)(2,1)} %get-tuple-element.149) | copy-start | bytes 16588804 | tf_op jit(solution)/shard_map/while
  101.1 4.4 %copy-start.2 = (bf16[75,36864]{1,0:T(8,128)(2,1)S(1)}, bf16[75,36864]{1,0:T(8,128)(2,1)}, u32[]{:S(2)}) copy-start(bf16[75,36864]{1,0:T(8,128)(2,1)} %get-tuple-element.149) | copy-start | bytes 16588804 | tf_op jit(solution)/shard_map/while
  109.8 4.4 %copy-start.2 = (bf16[75,36864]{1,0:T(8,128)(2,1)S(1)}, bf16[75,36864]{1,0:T(8,128)(2,1)}, u32[]{:S(2)}) copy-start(bf16[75,36864]{1,0:T(8,128)(2,1)} %get-tuple-element.149) | copy-start | bytes 16588804 | tf_op jit(solution)/shard_map/while
  118.5 4.4 %copy-start.2 = (bf16[75,36864]{1,0:T(8,128)(2,1)S(1)}, bf16[75,36864]{1,0:T(8,128)(2,1)}, u32[]{:S(2)}) copy-start(bf16[75,36864]{1,0:T(8,128)(2,1)} %get-tuple-element.149) | copy-start | bytes 16588804 | tf_op jit(solution)/shard_map/while
  127.2 4.4 %copy-start.2 = (bf16[75,36864]{1,0:T(8,128)(2,1)S(1)}, bf16[75,36864]{1,0:T(8,128)(2,1)}, u32[]{:S(2)}) copy-start(bf16[75,36864]{1,0:T(8,128)(2,1)} %get-tuple-element.149) | copy-start | bytes 16588804 | tf_op jit(solution)/shard_map/while
  135.9 4.4 %copy-start.2 = (bf16[75,36864]{1,0:T(8,128)(2,1)S(1)}, bf16[75,36864]{1,0:T(8,128)(2,1)}, u32[]{:S(2)}) copy-start(bf16[75,36864]{1,0:T(8,128)(2,1)} %get-tuple-element.149) | copy-start | bytes 16588804 | tf_op jit(solution)/shard_map/while
  144.6 4.4 %copy-start.2 = (bf16[75,36864]{1,0:T(8,128)(2,1)S(1)}, bf16[75,36864]{1,0:T(8,128)(2,1)}, u32[]{:S(2)}) copy-start(bf16[75,36864]{1,0:T(8,128)(2,1)} %get-tuple-element.149) | copy-start | bytes 16588804 | tf_op jit(solution)/shard_map/while
  153.3 4.4 %copy-start.2 = (bf16[75,36864]{1,0:T(8,128)(2,1)S(1)}, bf16[75,36864]{1,0:T(8,128)(2,1)}, u32[]{:S(2)}) copy-start(bf16[75,36864]{1,0:T(8,128)(2,1)} %get-tuple-element.149) | copy-start | bytes 16588804 | tf_op jit(solution)/shard_map/while
  161.9 4.4 %copy-start.2 = (bf16[75,36864]{1,0:T(8,128)(2,1)S(1)}, bf16[75,36864]{1,0:T(8,128)(2,1)}, u32[]{:S(2)}) copy-start(bf16[75,36864]{1,0:T(8,128)(2,1)} %get-tuple-element.149) | copy-start | bytes 16588804 | tf_op jit(solution)/shard_map/while
  170.6 4.4 %copy-start.2 = (bf16[75,36864]{1,0:T(8,128)(2,1)S(1)}, bf16[75,36864]{1,0:T(8,128)(2,1)}, u32[]{:S(2)}) copy-start(bf16[75,36864]{1,0:T(8,128)(2,1)} %get-tuple-element.149) | copy-start | bytes 16588804 | tf_op jit(solution)/shard_map/while
  179.3 4.4 %copy-start.2 = (bf16[75,36864]{1,0:T(8,128)(2,1)S(1)}, bf16[75,36864]{1,0:T(8,128)(2,1)}, u32[]{:S(2)}) copy-start(bf16[75,36864]{1,0:T(8,128)(2,1)} %get-tuple-element.149) | copy-start | bytes 16588804 | tf_op jit(solution)/shard_map/while
  188.0 4.4 %copy-start.2 = (bf16[75,36864]{1,0:T(8,128)(2,1)S(1)}, bf16[75,36864]{1,0:T(8,128)(2,1)}, u32[]{:S(2)}) copy-start(bf16[75,36864]{1,0:T(8,128)(2,1)} %get-tuple-element.149) | copy-start | bytes 16588804 | tf_op jit(solution)/shard_map/while
  196.7 4.4 %copy-start.2 = (bf16[75,36864]{1,0:T(8,128)(2,1)S(1)}, bf16[75,36864]{1,0:T(8,128)(2,1)}, u32[]{:S(2)}) copy-start(bf16[75,36864]{1,0:T(8,128)(2,1)} %get-tuple-element.149) | copy-start | bytes 16588804 | tf_op jit(solution)/shard_map/while
  205.4 4.4 %copy-start.2 = (bf16[75,36864]{1,0:T(8,128)(2,1)S(1)}, bf16[75,36864]{1,0:T(8,128)(2,1)}, u32[]{:S(2)}) copy-start(bf16[75,36864]{1,0:T(8,128)(2,1)} %get-tuple-element.149) | copy-start | bytes 16588804 | tf_op jit(solution)/shard_map/while
  214.1 4.4 %copy-start.2 = (bf16[75,36864]{1,0:T(8,128)(2,1)S(1)}, bf16[75,36864]{1,0:T(8,128)(2,1)}, u32[]{:S(2)}) copy-start(bf16[75,36864]{1,0:T(8,128)(2,1)} %get-tuple-element.149) | copy-start | bytes 16588804 | tf_op jit(solution)/shard_map/while
  222.9 28.6 %collective-permute-start.1 = (f32[64,16,256]{2,1,0:T(8,128)S(1)}, f32[64,16,256]{2,1,0:T(8,128)}, u32[]{:S(2)}, u32[]{:S(2)}) collective-permute-start(f32[64,16,256]{2,1,0:T(8,128)S(1)} %all-to-all-done.2), channel_id=1, source_target_pairs={{0,64},{1,65},{2,66},{3,67},{4,68},{5,69},{6,70},{7,71},{8,72},{9,... | collective-permute-start | bytes 3145736 | tf_op jit(solution)/shard_map/ppermute | solution.py:14
  224.6 8.0 %copy-start.3 = (bf16[128,8,32,128]{3,2,1,0:T(8,128)(2,1)S(1)}, bf16[128,8,32,128]{3,2,1,0:T(8,128)(2,1)}, u32[]{:S(2)}) copy-start(bf16[128,8,32,128]{3,2,1,0:T(8,128)(2,1)} %copy.71) | copy-start | bytes 25165828
where the time goes:
time: 275 us; the launch traced here: 272 us
  local copies, waits for them, and re-layouts  108 us (39%)
  matrix products  107 us (39%)
  starting transfers between devices  32.1 us (12%)
  other arithmetic  17.5 us (6%)
  waiting for transfers between devices  7.11 us (3%)
    while x48, local copies, waits for them, and re-layouts  70.2 us
    dot_general x16, matrix products, advance(): lax.dot_general(operator, current, (((0,), (0,)), ((), ())), preferred_el...  68.8 us
    unnamed x26, local copies, waits for them, and re-layouts  18.3 us
    dot_general x1, matrix products, body(): jnp.dot(surf_write[0], forcing, precision=lax.Precision.HIGHEST)  12.9 us
    all_to_all x1, starting transfers between devices, body(): lax.all_to_all(targets, 'tile', split_axis=0, concat_axis=0, tiled=True)  12 us
    all_to_all x1, starting transfers between devices, body(): lax.all_to_all(partial_flux, 'tile', split_axis=0, concat_axis=0, tiled=T...  9.97 us
    dot_general x1, matrix products, backward_remap(): jnp.einsum('sjq,snq->snj', paired_weights, upper, preferred_element_type=...  8 us
    scatter-add x1, other arithmetic, body(): jax.ops.segment_sum(arriving.reshape(slot_count, NF * BLK), position, num...  6.68 us
  transfers between devices with their start and end apart: 5, of which 2 were waited for; matrix products, arithmetic and copies ran while one was open for 66% of the time, Pallas kernels for 0%

commit v1 on v0

v1 whole, which is shorter than its diff:
```python
import jax
import jax.numpy as jnp
from jax import lax
from jax.experimental import pallas as pl
from jax.experimental.pallas import tpu as pltpu
from jax.sharding import PartitionSpec as P

NF = 4
BLK = 64
NSTEP = 16
LANES = 128
GROUP = 8
BF16 = jnp.bfloat16
F32 = jnp.float32


def lanes_below(shape, edge):
    return lax.broadcasted_iota(jnp.int32, shape, len(shape) - 1) < edge


def surface_kernel(read_ref, state_ref, out_ref, held):
    step = pl.program_id(0)
    width = state_ref.shape[1]
    tiles = width // LANES
    fields = jnp.dot(read_ref[...], state_ref[...], preferred_element_type=F32)
    for tile in range(tiles):
        row = pl.multiple_of((step * tiles + tile) * 8, 8)
        held[pl.ds(row, NF), :] = fields[:, tile * LANES : (tile + 1) * LANES]

    @pl.when(step == pl.num_programs(0) - 1)
    def _():
        pairs = out_ref.shape[0] // 2
        left = lanes_below((pairs, LANES), BLK)
        for duo in range(NF // 2):
            first = held[pl.ds(2 * duo, pairs, stride=8), :]
            second = held[pl.ds(2 * duo + 1, pairs, stride=8), :]
            cols = slice(duo * LANES, (duo + 1) * LANES)
            even = jnp.where(left, first, pltpu.roll(second, BLK, 1))
            odd = jnp.where(left, pltpu.roll(first, BLK, 1), second)
            out_ref[:pairs, cols] = even.astype(BF16)
            out_ref[pairs:, cols] = odd.astype(BF16)


def surface_blocks(read, state, width=4096):
    levels, cells = state.shape
    blocks = cells // BLK
    return pl.pallas_call(
        surface_kernel,
        grid=(cells // width,),
        out_shape=jax.ShapeDtypeStruct((blocks, NF * BLK), BF16),
        in_specs=[
            pl.BlockSpec((NF, levels), lambda i: (0, 0)),
            pl.BlockSpec((levels, width), lambda i: (0, i)),
        ],
        out_specs=pl.BlockSpec((blocks, NF * BLK), lambda i: (0, 0)),
        scratch_shapes=[pltpu.VMEM((blocks // 2 * 8, LANES), F32)],
        name="surface",
    )(read, state)


def fill_spread(spread):
    row = lax.broadcasted_iota(jnp.int32, spread.shape, 0)
    col = lax.broadcasted_iota(jnp.int32, spread.shape, 1)
    source = (col >> 10) * BLK + ((col >> 4) & 15) * 4 + ((col >> 8) & 3)
    spread[...] = jnp.where(row == source, 1.0, 0.0).astype(BF16)


def own_slot(rows, cols):
    row = lax.broadcasted_iota(jnp.int32, (rows, cols), 0)
    col = lax.broadcasted_iota(jnp.int32, (rows, cols), 1)
    return (row & 15) == (col & 15)


def stacked_weights(weights_ref, tile):
    width = 4 * BLK
    return jnp.concatenate(
        [weights_ref[tile, :, q * width : (q + 1) * width] for q in range(BLK // 4)], 0
    )


def outgoing_kernel(section_ref, key_ref, table_ref, blocks_ref, weights_ref, out_ref, spread):
    step = pl.program_id(0)
    rows = LANES
    blocks = blocks_ref.shape[0]
    key = jnp.broadcast_to(key_ref[pl.ds(step, 1), :], (rows, rows)).T
    pieces = []
    for start in range(0, blocks, LANES):
        stop = min(start + LANES, blocks)
        piece = jnp.where(key == table_ref[:, start : start + LANES], 1.0, 0.0).astype(BF16)
        pieces.append(piece[:, : stop - start])
    chosen = jnp.dot(
        jnp.concatenate(pieces, 1), blocks_ref[...], preferred_element_type=F32
    ).astype(BF16)

    @pl.when(section_ref[0] == 0)
    def _():
        out_ref[...] = chosen

    @pl.when(section_ref[0] == 1)
    def _():
        @pl.when(step == 0)
        def _():
            fill_spread(spread)

        mine = own_slot(rows, spread.shape[1])
        spaced = []
        for duo in range(NF // 2):
            wide = jnp.dot(
                chosen[:, duo * LANES : (duo + 1) * LANES], spread[...], preferred_element_type=F32
            )
            spaced.append(jnp.where(mine, wide, 0.0).astype(BF16))
        left = lanes_below((16, LANES), BLK)
        for tile in range(GROUP):
            slots = slice(tile * 16, (tile + 1) * 16)
            operand = jnp.concatenate(
                [
                    spaced[duo][slots, part * 256 : (part + 1) * 256]
                    for duo in range(NF // 2)
                    for part in range(8)
                ],
                0,
            )
            product = jnp.dot(
                operand, stacked_weights(weights_ref, tile), preferred_element_type=F32
            )
            sums = []
            for field in range(NF):
                quarter = [
                    product[field * 64 + k * 16 : field * 64 + (k + 1) * 16] for k in range(4)
                ]
                total = jnp.where(left, quarter[0][:, :LANES], quarter[1][:, :LANES]) + jnp.where(
                    left, quarter[2][:, LANES:], quarter[3][:, LANES:]
                )
                sums.append(total + pltpu.roll(total, BLK, 1))
            for duo in range(NF // 2):
                out_ref[slots, duo * LANES : (duo + 1) * LANES] = jnp.where(
                    left, sums[2 * duo], sums[2 * duo + 1]
                ).astype(BF16)


def outgoing(section, key, table, blocks, weights):
    lists, cap, square = weights.shape
    slots = lists * cap
    count, width = blocks.shape
    return pl.pallas_call(
        outgoing_kernel,
        out_shape=jax.ShapeDtypeStruct((slots, width), BF16),
        grid_spec=pltpu.PrefetchScalarGridSpec(
            num_scalar_prefetch=1,
            grid=(lists // GROUP,),
            in_specs=[
                pl.BlockSpec(key.shape, lambda i, sec: (0, 0)),
                pl.BlockSpec(table.shape, lambda i, sec: (0, 0)),
                pl.BlockSpec((count, width), lambda i, sec: (0, 0)),
                pl.BlockSpec((GROUP, cap, square), lambda i, sec: (i * sec[0], 0, 0)),
            ],
            out_specs=pl.BlockSpec((GROUP * cap, width), lambda i, sec: (i, 0)),
            scratch_shapes=[pltpu.VMEM((LANES, 2048), BF16)],
        ),
        name="outgoing",
    )(section, key, table, blocks, weights)


def incoming_kernel(
    section_ref, key_ref, table_ref, arrived_ref, weights_ref, out_ref, spread, masked, terms
):
    step = pl.program_id(0)
    rows = LANES
    here = pl.ds(pl.multiple_of(step * rows, rows), rows)

    @pl.when(section_ref[0] == 1)
    def _():
        terms[here, :] = arrived_ref[...]

    @pl.when(section_ref[0] == 0)
    def _():
        @pl.when(step == 0)
        def _():
            fill_spread(spread)

        left = lanes_below((rows, LANES), BLK)
        low, high = [], []
        for duo in range(NF // 2):
            both = arrived_ref[:, duo * LANES : (duo + 1) * LANES].astype(F32)
            turned = pltpu.roll(both, BLK, 1)
            low += [jnp.where(left, both, 0.0).astype(BF16), jnp.where(left, turned, 0.0).astype(BF16)]
            high += [jnp.where(left, 0.0, turned).astype(BF16), jnp.where(left, 0.0, both).astype(BF16)]
        blank = jnp.zeros((16, LANES), BF16)
        mine = own_slot(256, 256)
        for tile in range(GROUP):
            slots = slice(tile * 16, (tile + 1) * 16)
            lines = []
            for field in range(NF):
                lo, hi = low[field][slots], high[field][slots]
                lines += [
                    jnp.concatenate([lo, blank], 1),
                    jnp.concatenate([hi, blank], 1),
                    jnp.concatenate([blank, lo], 1),
                    jnp.concatenate([blank, hi], 1),
                ]
            product = lax.dot_general(
                jnp.concatenate(lines, 0),
                stacked_weights(weights_ref, tile),
                (((1,), (1,)), ((), ())),
                preferred_element_type=F32,
            )
            kept = jnp.where(mine, product, 0.0).astype(BF16)
            for part in range(4 * NF):
                masked[slots, part * 256 : (part + 1) * 256] = kept[part * 16 : (part + 1) * 16]
        for duo in range(NF // 2):
            terms[here, duo * LANES : (duo + 1) * LANES] = lax.dot_general(
                masked[:, duo * 2048 : (duo + 1) * 2048],
                spread[...],
                (((1,), (1,)), ((), ())),
                preferred_element_type=F32,
            ).astype(BF16)

    @pl.when(step == pl.num_programs(0) - 1)
    def _():
        slots = terms.shape[0]
        count = out_ref.shape[0] // 4
        table = jnp.broadcast_to(table_ref[...], (LANES, table_ref.shape[1])).T[:count]
        picks = [
            jnp.where(table == key_ref[r : r + 1, :], 1.0, 0.0).astype(BF16)
            for r in range(slots // LANES)
        ]
        total = jnp.dot(jnp.concatenate(picks, 1), terms[...], preferred_element_type=F32)
        pairs = count // 2
        left = lanes_below((pairs, LANES), BLK)
        for duo in range(NF // 2):
            even = total[:pairs, duo * LANES : (duo + 1) * LANES]
            odd = total[pairs:, duo * LANES : (duo + 1) * LANES]
            fields = (
                jnp.where(left, even, pltpu.roll(odd, BLK, 1)),
                jnp.where(left, pltpu.roll(even, BLK, 1), odd),
            )
            for n, field in enumerate(fields):
                coarse = field.astype(BF16).astype(F32)
                out_ref[pl.ds(2 * duo + n, pairs, stride=8), :] = coarse
                out_ref[pl.ds(NF + 2 * duo + n, pairs, stride=8), :] = field - coarse


def incoming(section, key, table, arrived, weights, blocks):
    lists, cap, square = weights.shape
    slots, width = arrived.shape
    return pl.pallas_call(
        incoming_kernel,
        out_shape=jax.ShapeDtypeStruct((blocks // 2 * 8, LANES), F32),
        grid_spec=pltpu.PrefetchScalarGridSpec(
            num_scalar_prefetch=1,
            grid=(lists // GROUP,),
            in_specs=[
                pl.BlockSpec(key.shape, lambda i, sec: (0, 0)),
                pl.BlockSpec(table.shape, lambda i, sec: (0, 0)),
                pl.BlockSpec((GROUP * cap, width), lambda i, sec: (i, 0)),
                pl.BlockSpec((GROUP, cap, square), lambda i, sec: (i * (1 - sec[0]), 0, 0)),
            ],
            out_specs=pl.BlockSpec((blocks // 2 * 8, LANES), lambda i, sec: (0, 0)),
            scratch_shapes=[
                pltpu.VMEM((LANES, 2048), BF16),
                pltpu.VMEM((GROUP * cap, 4096), BF16),
                pltpu.VMEM((slots, width), BF16),
            ],
        ),
        name="incoming",
    )(section, key, table, arrived, weights)


def sweep_kernel(ops_ref, state_ref, coef_ref, out_ref):
    current = state_ref[...]
    factors = coef_ref[...].astype(F32)
    for step in range(NSTEP):
        stepped = jnp.dot(ops_ref[step], current, preferred_element_type=F32)
        current = (stepped * factors).astype(BF16)
    out_ref[...] = current


def sweep(ops, state, coef, width=4096):
    levels, cells = state.shape
    return pl.pallas_call(
        sweep_kernel,
        grid=(cells // width,),
        out_shape=jax.ShapeDtypeStruct((levels, cells), BF16),
        in_specs=[
            pl.BlockSpec(ops.shape, lambda i: (0, 0, 0)),
            pl.BlockSpec((levels, width), lambda i: (0, i)),
            pl.BlockSpec((levels, width), lambda i: (0, i)),
        ],
        out_specs=pl.BlockSpec((levels, width), lambda i: (0, i)),
        compiler_params=pltpu.CompilerParams(vmem_limit_bytes=48 << 20),
        name="sweep",
    )(ops, state, coef)


def finish_kernel(write_ref, forcing_ref, swept_ref, out_ref):
    tiles = swept_ref.shape[1] // LANES
    forcing = jnp.concatenate([forcing_ref[t * 8 : (t + 1) * 8, :] for t in range(tiles)], 1)
    operand = jnp.concatenate([forcing, forcing], 0).astype(BF16)
    added = jnp.dot(write_ref[...], operand, preferred_element_type=F32)
    out_ref[...] = (swept_ref[...].astype(F32) + added).astype(BF16)


def finish(write, forcing, swept, width=4096):
    levels, cells = swept.shape
    return pl.pallas_call(
        finish_kernel,
        grid=(cells // width,),
        out_shape=jax.ShapeDtypeStruct((levels, cells), BF16),
        in_specs=[
            pl.BlockSpec(write.shape, lambda i: (0, 0)),
            pl.BlockSpec((width // LANES * 8, LANES), lambda i: (i, 0)),
            pl.BlockSpec((levels, width), lambda i: (0, i)),
        ],
        out_specs=pl.BlockSpec((levels, width), lambda i: (0, i)),
        name="finish",
    )(write, forcing, swept)


def body(
    adjoint_state,
    tangent_coef,
    column_ops,
    surf_read,
    surf_write,
    remap_weights,
    pair_atmos,
    pair_ocean,
    list_len,
    ocean_owned,
):
    section = lax.axis_index("sec")
    lists, cap = pair_atmos.shape[1:]
    blocks = ocean_owned.shape[1]
    pairs = blocks // 2
    state = adjoint_state[0]
    arrived_ids = lax.all_to_all(pair_ocean[0], "tile", split_axis=0, concat_axis=0, tiled=True)

    surface = surface_blocks(surf_read[0], state)
    partner = lax.ppermute(surface, "sec", [(0, 1), (1, 0)])

    live = lax.broadcasted_iota(jnp.int32, (lists, cap), 1) < list_len[0][:, None]
    atmos = pair_atmos[0]
    atmos_key = jnp.where(live, (atmos & 1) * pairs + (atmos >> 1), -1)
    keys = (lists * cap // LANES, LANES)
    atmos_key = atmos_key.reshape(keys).astype(F32)
    ocean_key = arrived_ids.reshape(keys).astype(F32)
    padded = -(-blocks // LANES) * LANES
    owned = jnp.pad(ocean_owned[0].reshape(pairs, 2).T.reshape(1, blocks), ((0, 0), (0, padded - blocks)), constant_values=-2)
    owned_table = owned.astype(F32)
    plain_table = lax.broadcasted_iota(jnp.int32, (1, padded), 1).astype(F32)
    first = section == 0
    out_key = jnp.where(first, ocean_key, atmos_key)
    in_key = jnp.where(first, atmos_key, ocean_key)
    out_table = jnp.where(first, owned_table, plain_table)
    in_table = jnp.where(first, plain_table, owned_table)
    which = section.reshape(1).astype(jnp.int32)

    payload = outgoing(which, out_key, out_table, partner, remap_weights[0])
    received = lax.all_to_all(
        payload.reshape(lists, cap, NF * BLK), "tile", split_axis=0, concat_axis=0, tiled=True
    )
    swept = sweep(column_ops[0].transpose(0, 2, 1), state, tangent_coef[0])
    forcing = incoming(
        which, in_key, in_table, received.reshape(lists * cap, NF * BLK), remap_weights[0], blocks
    )
    write = surf_write[0]
    coarse = lax.reduce_precision(write, 8, 7)
    fine = write - coarse
    operand = jnp.concatenate([coarse, coarse, fine, fine], 1).astype(BF16)
    return finish(operand, forcing, swept)[None]


def solution(mesh):
    in_specs = (
        P("sec", None, "tile"),
        P("sec", None, "tile"),
        P("sec", None, None, None),
        P("sec", None, None),
        P("sec", None, None),
        P("tile", None, None, None),
        P("tile", None, None),
        P("tile", None, None),
        P("tile", None),
        P("tile", None),
    )
    out_specs = P("sec", None, "tile")
    return jax.shard_map(body, mesh=mesh, in_specs=in_specs, out_specs=out_specs, check_vma=False)
```

time: 275 us -> 95.8 us (0.35)
  matrix products: 107 us -> 0 us
  local copies, waits for them, and re-layouts: 108 us -> 7.99 us
  Pallas kernels: 0 us -> 61.7 us
  other arithmetic: 17.5 us -> 2.03 us
  starting transfers between devices: 32.1 us -> 23 us
  waiting for transfers between devices: 7.11 us -> 0.01 us
    dot_general x22 -> x0, matrix products: 107 us -> none  [the longest x16 68.8 us: advance(): lax.dot_general(operator, current, (((0,), (0,)), ((), ())), preferred_el...]
    while x49 -> x0, local copies, waits for them, and re-layouts: 70.3 us -> none
    pallas_call x0 -> x5, Pallas kernels: none -> 61.7 us  [the longest x1 27.8 us: sweep(): pl.pallas_call(sweep_kernel, grid=(cells // width,), out_shape=jax.ShapeD...]
    scatter-add x2 -> x0, other arithmetic: 13.1 us -> none  [the longest x1 6.68 us: body(): jax.ops.segment_sum(arriving.reshape(slot_count, NF * BLK), position, num...]
    unnamed x26 -> x19, local copies, waits for them, and re-layouts: 18.3 us -> 6.41 us
    gather x3 -> x0, local copies, waits for them, and re-layouts: 8.31 us -> none  [the longest x2 4.37 us: body(): picked = surface_blocks[source]]
    all_to_all x3 -> x2, waiting for transfers between devices: 6.34 us -> 0.01 us  [the longest x1 0.01 us: body(): lax.all_to_all(payload.reshape(lists, cap, NF * BLK), 'tile', split_axis=...]
    all_to_all x3 -> x2, starting transfers between devices: 26.6 us -> 22 us  [the longest x1 12 us: body(): lax.all_to_all(pair_ocean[0], 'tile', split_axis=0, concat_axis=0, tiled=...]
  transfers between devices with their start and end apart: 5 -> 3, of which waited for: 2 -> 0; matrix products, arithmetic and copies ran while one was open for 66% -> 5% of each run, Pallas kernels for 0% -> 37%
where the time goes in v1:
time: 95.8 us; the launch traced here: 94.8 us
  Pallas kernels  61.7 us (64%)
  starting transfers between devices  23 us (24%)
  local copies, waits for them, and re-layouts  7.99 us (8%)
  other arithmetic  2.03 us (2%)
    pallas_call x1, Pallas kernels, sweep(): pl.pallas_call(sweep_kernel, grid=(cells // width,), out_shape=jax.ShapeD...  27.8 us
    all_to_all x1, starting transfers between devices, body(): lax.all_to_all(pair_ocean[0], 'tile', split_axis=0, concat_axis=0, tiled=...  12 us
    pallas_call x1, Pallas kernels, outgoing(): pl.pallas_call(outgoing_kernel, out_shape=jax.ShapeDtypeStruct((slots, wi...  11.3 us
    all_to_all x1, starting transfers between devices, body(): lax.all_to_all(payload.reshape(lists, cap, NF * BLK), 'tile', split_axis=...  10.1 us
    pallas_call x1, Pallas kernels, finish(): pl.pallas_call(finish_kernel, grid=(cells // width,), out_shape=jax.Shape...  9.62 us
    pallas_call x1, Pallas kernels, surface_blocks(): pl.pallas_call(surface_kernel, grid=(cells // width,), out_shape=jax.Shap...  7.46 us
    unnamed x19, local copies, waits for them, and re-layouts  6.41 us
    pallas_call x1, Pallas kernels, incoming(): pl.pallas_call(incoming_kernel, out_shape=jax.ShapeDtypeStruct((blocks //...  5.53 us
  transfers between devices with their start and end apart: 3, of which 0 were waited for; matrix products, arithmetic and copies ran while one was open for 5% of the time, Pallas kernels for 37%

profile of v1, /device:TPU:1, one launch (start us, length us, event | category | flops | bytes accessed | tf_op | source)
XLA Modules:
  0.0 94.8 jit_solution(8055191511752405342)
XLA Ops:
  0.0 0.0 copy-start.5
  0.0 0.0 copy-start.4
  0.0 0.0 copy-start.7
  0.0 1.4 %copy.22 = s32[1,64,16]{2,1,0:T(8,128)} copy(s32[1,64,16]{1,2,0:T(8,128)} %param.17) | data formatting | bytes 8192 | tf_op args[7]
  1.4 12.0 %all-to-all-start = ((s32[64,1,16]{2,1,0:T(1,128)}), s32[64,1,16]{2,1,0:T(1,128)S(1)}, u32[]{:S(2)}, u32[]{:S(2)}) async-start(s32[64,1,16]{2,1,0:T(1,128)} %bitcast.2), calls=%async_computation | async-start | bytes 65536 | tf_op jit(solution)/shard_map/all_to_all | solution.py:336
  13.4 7.5 %surface.1 = bf16[576,256]{1,0:T(8,128)(2,1)} custom-call(bf16[4,75]{1,0:T(4,128)(2,1)} %bitcast.25, bf16[75,36864]{1,0:T(8,128)(2,1)} %bitcast.19), custom_call_target="tpu_custom_call" | custom-call | tf_op jit(solution)/shard_map/surface/pallas_call | solution.py:47
  20.8 0.0 copy-start.6
  20.9 0.0 copy-start.2
  20.9 1.0 %collective-permute-start = (bf16[576,256]{1,0:T(8,128)(2,1)}, bf16[576,256]{1,0:T(8,128)(2,1)S(1)}, u32[]{:S(2)}, u32[]{:S(2)}) collective-permute-start(bf16[576,256]{1,0:T(8,128)(2,1)} %surface.1), channel_id=1, source_target_pairs={{0,64},{64,0},{1,65},{65,1},{2,66},{66,2},{3,67},{67,3},{4,68},{68... | collective-permute-start | bytes 884744 | tf_op jit(solution)/shard_map/ppermute | solution.py:339
  21.8 0.0 copy-done.5
  21.8 0.0 copy-done.4
  21.8 0.1 reshape_squeeze.3
  22.0 0.1 copy.23
  22.1 0.1 reshape.41
  22.2 0.7 broadcast_select_fusion
  22.8 0.6 broadcast.27
  23.4 0.0 copy-done.7
  23.4 0.6 reduce.8
  24.0 0.1 lt.13
  24.1 0.1 iota.19
  24.2 0.1 copy.21
  24.3 0.1 add.10
  24.4 0.1 lt.14
  24.4 0.1 lt.15
  24.5 0.0 all-to-all-done
  24.5 0.1 convert_reduce_fusion
  24.6 0.1 convert_element_type.28
  24.7 0.6 convert_select_fusion
  25.3 0.0 collective-permute-done.blocks_ref
  25.3 0.0 copy-start.3
  25.3 0.7 copy-done.3
  26.0 11.3 %outgoing.1 = bf16[1024,256]{1,0:T(8,128)(2,1)} custom-call(s32[1]{0:T(128)} %bitcast.1.section_ref, f32[8,128]{1,0:T(8,128)} %get-tuple-element.5.key_ref, f32[1,640]{1,0:T(1,128)} %get-tuple-element.7.table_ref, bf16[576,256]{1,0:T(8,128)(2,1)} %copy-done.3, bf16[64,16,4096]{2,1,0:T(8,128)(2,1)} %bitcast.17), custom_call_target="tpu_custom_call" | custom-call | tf_op jit(solution)/shard_map/outgoing/pallas_call | solution.py:145
  37.3 10.1 %all-to-all-start.1 = ((bf16[64,16,256]{2,1,0:T(8,128)(2,1)}), bf16[64,16,256]{2,1,0:T(8,128)(2,1)S(1)}, u32[]{:S(2)}, u32[]{:S(2)}) async-start(bf16[64,16,256]{2,1,0:T(8,128)(2,1)} %bitcast.22), calls=%async_computation.1 | async-start | bytes 1048576 | tf_op jit(solution)/shard_map/all_to_all | solution.py:359
  47.4 0.0 copy-done.6
  47.4 0.7 copy.25.write_ref
  48.2 0.0 copy-done.2
  48.2 0.4 copy.24
  48.5 27.8 %sweep.1.swept_ref = bf16[75,36864]{1,0:T(8,128)(2,1)S(1)} custom-call(bf16[16,75,75]{2,1,0:T(8,128)(2,1)S(1)} %bitcast.16, bf16[75,36864]{1,0:T(8,128)(2,1)} %bitcast.20, bf16[75,36864]{1,0:T(8,128)(2,1)} %bitcast.21), custom_call_target="tpu_custom_call" | custom-call | tf_op jit(solution)/shard_map/sweep/pallas_call | solution.py:280
  76.4 0.0 copy-start
  76.4 2.5 %copy-done = bf16[75,36864]{1,0:T(8,128)(2,1)} copy-done((bf16[75,36864]{1,0:T(8,128)(2,1)}, bf16[75,36864]{1,0:T(8,128)(2,1)S(1)}, u32[]{:S(2)}) %copy-start) | copy-done | bytes 5529624
  78.9 0.0 all-to-all-done.1
  78.9 0.0 copy-start.1
  78.9 0.8 copy-done.1
  79.7 5.5 %incoming.1.forcing_ref = f32[2304,128]{1,0:T(8,128)} custom-call(s32[1]{0:T(128)} %bitcast.1.section_ref, f32[8,128]{1,0:T(8,128)} %get-tuple-element.6.key_ref, f32[1,640]{1,0:T(1,128)} %get-tuple-element.8.table_ref, bf16[1024,256]{1,0:T(8,128)(2,1)} %bitcast.23, bf16[64,16,4096]{2,1,0:T(8,128)(2,1)} %bitcast.18), custom_call_target="tpu_custom_call" | custom-call | tf_op jit(solution)/shard_map/incoming/pallas_call | solution.py:246
  85.2 9.6 %finish.1 = bf16[75,36864]{1,0:T(8,128)(2,1)} custom-call(bf16[75,16]{1,0:T(8,128)(2,1)} %copy.25.write_ref, f32[2304,128]{1,0:T(8,128)} %incoming.1.forcing_ref, bf16[75,36864]{1,0:T(8,128)(2,1)} %copy-done), custom_call_target="tpu_custom_call" | custom-call | tf_op jit(solution)/shard_map/finish/pallas_call | solution.py:305
  (5 shorter events, 0.0 us)
Async XLA Ops:
  0.0 21.8 %copy-start.5 = (s32[1,576]{1,0:T(1,128)S(1)}, s32[1,576]{1,0:T(1,128)}, u32[]{:S(2)}) copy-start(s32[1,576]{1,0:T(1,128)} %param.19) | copy-start | bytes 6916
  0.0 21.8 %copy-start.4 = (s32[1,64,16]{1,2,0:T(8,128)S(1)}, s32[1,64,16]{1,2,0:T(8,128)}, u32[]{:S(2)}) copy-start(s32[1,64,16]{1,2,0:T(8,128)} %param.16) | copy-start | bytes 12292
  0.0 23.4 %copy-start.7 = (s32[1,64]{1,0:T(1,128)S(1)}, s32[1,64]{1,0:T(1,128)}, u32[]{:S(2)}) copy-start(s32[1,64]{1,0:T(1,128)} %param.18) | copy-start | bytes 772
  1.4 23.1 %all-to-all-start = ((s32[64,1,16]{2,1,0:T(1,128)}), s32[64,1,16]{2,1,0:T(1,128)S(1)}, u32[]{:S(2)}, u32[]{:S(2)}) async-start(s32[64,1,16]{2,1,0:T(1,128)} %bitcast.2), calls=%async_computation | async-start | bytes 65536 | tf_op jit(solution)/shard_map/all_to_all | solution.py:336
  20.8 26.6 %copy-start.6 = (f32[1,75,4]{1,2,0:T(4,128)S(1)}, f32[1,75,4]{1,2,0:T(4,128)}, u32[]{:S(2)}) copy-start(f32[1,75,4]{1,2,0:T(4,128)} %param.14) | copy-start | bytes 3604
  20.9 27.3 %copy-start.2 = (bf16[1,16,75,75]{3,1,2,0:T(8,128)(2,1)S(1)}, bf16[1,16,75,75]{3,1,2,0:T(8,128)(2,1)}, u32[]{:S(2)}) copy-start(bf16[1,16,75,75]{3,1,2,0:T(8,128)(2,1)} %param.12) | copy-start | bytes 540004
  20.9 4.5 %collective-permute-start = (bf16[576,256]{1,0:T(8,128)(2,1)}, bf16[576,256]{1,0:T(8,128)(2,1)S(1)}, u32[]{:S(2)}, u32[]{:S(2)}) collective-permute-start(bf16[576,256]{1,0:T(8,128)(2,1)} %surface.1), channel_id=1, source_target_pairs={{0,64},{64,0},{1,65},{65,1},{2,66},{66,2},{3,67},{67,3},{4,68},{68... | collective-permute-start | bytes 884744 | tf_op jit(solution)/shard_map/ppermute | solution.py:339
  25.3 0.7 copy-start.3
  37.3 41.5 %all-to-all-start.1 = ((bf16[64,16,256]{2,1,0:T(8,128)(2,1)}), bf16[64,16,256]{2,1,0:T(8,128)(2,1)S(1)}, u32[]{:S(2)}, u32[]{:S(2)}) async-start(bf16[64,16,256]{2,1,0:T(8,128)(2,1)} %bitcast.22), calls=%async_computation.1 | async-start | bytes 1048576 | tf_op jit(solution)/shard_map/all_to_all | solution.py:359
  76.4 2.5 %copy-start = (bf16[75,36864]{1,0:T(8,128)(2,1)}, bf16[75,36864]{1,0:T(8,128)(2,1)S(1)}, u32[]{:S(2)}) copy-start(bf16[75,36864]{1,0:T(8,128)(2,1)S(1)} %sweep.1.swept_ref) | copy-start | bytes 16588804
  78.9 0.8 copy-start.1

commit v2 on v0

v2 whole, which is shorter than its diff:
```python
import jax
import jax.numpy as jnp
from jax import lax
from jax.experimental import pallas as pl
from jax.experimental.pallas import tpu as pltpu
from jax.sharding import PartitionSpec as P

NF = 4
BLK = 64
NSTEP = 16
LANES = 128
GROUP = 8
SPLIT = 2048
STRIDE = 3 * SPLIT
VMEM_LIMIT = 56 << 20
BF16 = jnp.bfloat16
F32 = jnp.float32


def lanes_below(shape, edge):
    return lax.broadcasted_iota(jnp.int32, shape, len(shape) - 1) < edge


def surface_kernel(read_ref, state_hbm, out_ref, state, held, sems):
    parts = sems.shape[0]
    width = state.shape[1] // parts
    tiles = width // LANES

    def fetch(part):
        cols = pl.ds(pl.multiple_of(part * width, width), width)
        return pltpu.make_async_copy(state_hbm.at[:, cols], state.at[:, cols], sems.at[part])

    for part in range(parts):
        fetch(part).start()

    def compute(part, carry):
        fetch(part).wait()
        cols = pl.ds(pl.multiple_of(part * width, width), width)
        fields = jnp.dot(read_ref[...], state[:, cols], preferred_element_type=F32)
        for tile in range(tiles):
            row = pl.multiple_of((part * tiles + tile) * 8, 8)
            held[pl.ds(row, NF), :] = fields[:, tile * LANES : (tile + 1) * LANES]
        return carry

    lax.fori_loop(0, parts, compute, 0)
    pairs = out_ref.shape[0] // 2
    left = lanes_below((pairs, LANES), BLK)
    for duo in range(NF // 2):
        first = held[pl.ds(2 * duo, pairs, stride=8), :]
        second = held[pl.ds(2 * duo + 1, pairs, stride=8), :]
        cols = slice(duo * LANES, (duo + 1) * LANES)
        even = jnp.where(left, first, pltpu.roll(second, BLK, 1))
        odd = jnp.where(left, pltpu.roll(first, BLK, 1), second)
        out_ref[:pairs, cols] = even.astype(BF16)
        out_ref[pairs:, cols] = odd.astype(BF16)


def surface_blocks(read, state, parts=9):
    levels, cells = state.shape
    blocks = cells // BLK
    return pl.pallas_call(
        surface_kernel,
        out_shape=jax.ShapeDtypeStruct((blocks, NF * BLK), BF16),
        in_specs=[
            pl.BlockSpec(memory_space=pltpu.VMEM),
            pl.BlockSpec(memory_space=pl.ANY),
        ],
        out_specs=pl.BlockSpec(memory_space=pltpu.VMEM),
        scratch_shapes=[
            pltpu.VMEM((levels, cells), BF16),
            pltpu.VMEM((blocks // 2 * 8, LANES), F32),
            pltpu.SemaphoreType.DMA((parts,)),
        ],
        compiler_params=pltpu.CompilerParams(vmem_limit_bytes=VMEM_LIMIT),
        name="surface",
    )(read, state)


def fetch_weights(weights_hbm, weights, sems, part):
    lists = pl.ds(part * GROUP, GROUP)
    return pltpu.make_async_copy(weights_hbm.at[lists], weights.at[lists], sems.at[part])


def half_list(weights, tile, half):
    return jnp.concatenate(
        [weights[tile, half, :, q * LANES : (q + 1) * LANES] for q in range(BLK // 2)], 0
    )


def pick(values, lanes):
    return jnp.take_along_axis(values, lanes, axis=1, mode="promise_in_bounds")


def outgoing_kernel(
    section_ref, key_ref, table_ref, blocks_ref, weights_hbm, out_ref, weights, chosen, sems
):
    parts = sems.shape[0]
    blocks = blocks_ref.shape[0]
    forward = section_ref[0] == 1

    @pl.when(forward)
    def _():
        for part in range(parts):
            fetch_weights(weights_hbm, weights, sems, part).start()

    for part in range(parts):
        key = jnp.broadcast_to(key_ref[part : part + 1, :], (LANES, LANES)).T
        pieces = []
        for start in range(0, blocks, LANES):
            stop = min(start + LANES, blocks)
            piece = jnp.where(key == table_ref[:, start : start + LANES], 1.0, 0.0).astype(BF16)
            pieces.append(piece[:, : stop - start])
        chosen[part * LANES : (part + 1) * LANES, :] = jnp.dot(
            jnp.concatenate(pieces, 1), blocks_ref[...], preferred_element_type=F32
        )

    @pl.when(jnp.logical_not(forward))
    def _():
        out_ref[...] = chosen[...].astype(BF16)

    @pl.when(forward)
    def _():
        lane = lax.broadcasted_iota(jnp.int32, (8, LANES), 1)
        row = lax.broadcasted_iota(jnp.int32, (8, LANES), 0)
        own = (lane & 7) == row
        left = lane < BLK

        def lists(part, carry):
            fetch_weights(weights_hbm, weights, sems, part).wait()
            for inner in range(GROUP):
                tile = part * GROUP + inner
                rows = pl.ds(pl.multiple_of(tile * 16, 16), 16)
                values = chosen[rows, :]
                results = []
                for half in range(2):
                    lines = []
                    for field in range(NF):
                        duo = values[
                            half * 8 : half * 8 + 8, field // 2 * LANES : (field // 2 + 1) * LANES
                        ]
                        for parity in range(2):
                            line = []
                            for side in range(2):
                                source = (field % 2) * BLK + 2 * (side * 16 + (lane >> 3)) + parity
                                line.append(jnp.where(own, pick(duo, source), 0.0))
                            lines.append(jnp.concatenate(line, 1))
                    product = jnp.dot(
                        jnp.concatenate(lines, 0).astype(BF16),
                        half_list(weights, tile, half),
                        preferred_element_type=F32,
                    )
                    sums = []
                    for field in range(NF):
                        even = product[field * 16 : field * 16 + 8]
                        odd = product[field * 16 + 8 : field * 16 + 16]
                        total = jnp.where(left, even, odd)
                        sums.append(total + pltpu.roll(total, BLK, 1))
                    results.append(
                        [jnp.where(left, sums[2 * duo], sums[2 * duo + 1]) for duo in range(NF // 2)]
                    )
                for duo in range(NF // 2):
                    out_ref[rows, duo * LANES : (duo + 1) * LANES] = jnp.concatenate(
                        [results[0][duo], results[1][duo]], 0
                    ).astype(BF16)
            return carry

        lax.fori_loop(0, parts, lists, 0)


def outgoing(section, key, table, blocks, weights):
    lists, halves, cap, square = weights.shape
    slots = lists * halves * cap
    width = blocks.shape[1]
    return pl.pallas_call(
        outgoing_kernel,
        out_shape=jax.ShapeDtypeStruct((slots, width), BF16),
        in_specs=[
            pl.BlockSpec(memory_space=pltpu.SMEM),
            pl.BlockSpec(memory_space=pltpu.VMEM),
            pl.BlockSpec(memory_space=pltpu.VMEM),
            pl.BlockSpec(memory_space=pltpu.VMEM),
            pl.BlockSpec(memory_space=pl.ANY),
        ],
        out_specs=pl.BlockSpec(memory_space=pltpu.VMEM),
        scratch_shapes=[
            pltpu.VMEM(weights.shape, BF16),
            pltpu.VMEM((slots, width), F32),
            pltpu.SemaphoreType.DMA((lists // GROUP,)),
        ],
        compiler_params=pltpu.CompilerParams(vmem_limit_bytes=VMEM_LIMIT),
        name="outgoing",
    )(section, key, table, blocks, weights)


def advance(ops_ref, states, coefs):
    current = jnp.concatenate([ref[...] for ref in states], 1)
    factors = jnp.concatenate([ref[...].astype(F32) for ref in coefs], 1)
    for step in range(NSTEP):
        stepped = jnp.dot(ops_ref[step], current, preferred_element_type=F32)
        current = (stepped * factors).astype(BF16)
    return current


def early_kernel(ops_ref, state_a, state_b, coef_a, coef_b, out_ref):
    out_ref[...] = advance(ops_ref, (state_a, state_b), (coef_a, coef_b))


def early_sweep(ops, state, coef):
    levels, cells = state.shape
    steps = cells // STRIDE // 2
    ratio = STRIDE // SPLIT
    first = pl.BlockSpec((levels, SPLIT), lambda i: (0, 2 * i * ratio))
    second = pl.BlockSpec((levels, SPLIT), lambda i: (0, (2 * i + 1) * ratio))
    return pl.pallas_call(
        early_kernel,
        grid=(steps,),
        out_shape=jax.ShapeDtypeStruct((levels, cells // ratio), BF16),
        in_specs=[pl.BlockSpec(ops.shape, lambda i: (0, 0, 0)), first, second, first, second],
        out_specs=pl.BlockSpec((levels, 2 * SPLIT), lambda i: (0, i)),
        compiler_params=pltpu.CompilerParams(vmem_limit_bytes=VMEM_LIMIT),
        name="early",
    )(ops, state, state, coef, coef)


def backward_lists(arrived_ref, weights_hbm, weights, terms, sems):
    lane = lax.broadcasted_iota(jnp.int32, (8, LANES), 1)
    row = lax.broadcasted_iota(jnp.int32, (8, LANES), 0)
    left = lane < BLK
    source = (((lane >> 1) & 15) << 3) + row
    half_kind = ((lane >> 5) & 1) * 2 + (lane & 1)

    def lists(part, carry):
        fetch_weights(weights_hbm, weights, sems, part).wait()
        for inner in range(GROUP):
            tile = part * GROUP + inner
            rows = pl.ds(pl.multiple_of(tile * 16, 16), 16)
            echoes = arrived_ref[rows, :].astype(F32)
            results = []
            for half in range(2):
                lines = []
                for duo in range(NF // 2):
                    both = echoes[half * 8 : half * 8 + 8, duo * LANES : (duo + 1) * LANES]
                    turned = pltpu.roll(both, BLK, 1)
                    lines += [
                        jnp.where(left, both, 0.0),
                        jnp.where(left, 0.0, turned),
                        jnp.where(left, turned, 0.0),
                        jnp.where(left, 0.0, both),
                    ]
                product = lax.dot_general(
                    jnp.concatenate(lines, 0).astype(BF16),
                    half_list(weights, tile, half),
                    (((1,), (1,)), ((), ())),
                    preferred_element_type=F32,
                )
                outs = []
                for duo in range(NF // 2):
                    fields = []
                    for field in (2 * duo, 2 * duo + 1):
                        total = None
                        for side in range(2):
                            for parity in range(2):
                                start = field * 16 + parity * 8
                                value = pick(
                                    product[start : start + 8, side * LANES : (side + 1) * LANES],
                                    source,
                                )
                                kind = side * 2 + parity
                                total = (
                                    value
                                    if total is None
                                    else jnp.where(half_kind == kind, value, total)
                                )
                        fields.append(total)
                    outs.append(jnp.where(left, fields[0], fields[1]))
                results.append(outs)
            for duo in range(NF // 2):
                terms[rows, duo * LANES : (duo + 1) * LANES] = jnp.concatenate(
                    [results[0][duo], results[1][duo]], 0
                ).astype(BF16)
        return carry

    lax.fori_loop(0, sems.shape[0], lists, 0)


def sum_terms(key_ref, table_ref, terms, forcing):
    slots = terms.shape[0]
    pairs = forcing.shape[0] // 8
    table = jnp.broadcast_to(table_ref[...], (LANES, table_ref.shape[1])).T[: 2 * pairs]
    picks = [
        jnp.where(table == key_ref[r : r + 1, :], 1.0, 0.0).astype(BF16)
        for r in range(slots // LANES)
    ]
    total = jnp.dot(jnp.concatenate(picks, 1), terms[...], preferred_element_type=F32)
    left = lanes_below((pairs, LANES), BLK)
    for duo in range(NF // 2):
        even = total[:pairs, duo * LANES : (duo + 1) * LANES]
        odd = total[pairs:, duo * LANES : (duo + 1) * LANES]
        fields = (
            jnp.where(left, even, pltpu.roll(odd, BLK, 1)),
            jnp.where(left, pltpu.roll(even, BLK, 1), odd),
        )
        for n, field in enumerate(fields):
            coarse = field.astype(BF16).astype(F32)
            forcing[pl.ds(2 * duo + n, pairs, stride=8), :] = coarse
            forcing[pl.ds(NF + 2 * duo + n, pairs, stride=8), :] = field - coarse


def late_kernel(
    section_ref,
    key_ref,
    table_ref,
    arrived_ref,
    weights_hbm,
    write_ref,
    ops_ref,
    swept_ref,
    state_a,
    state_b,
    coef_a,
    coef_b,
    out_ref,
    weights,
    terms,
    forcing,
    sems,
):
    step = pl.program_id(0)
    parts = sems.shape[0]

    @pl.when(step == 0)
    def _():
        @pl.when(section_ref[0] == 0)
        def _():
            for part in range(parts):
                fetch_weights(weights_hbm, weights, sems, part).start()
            backward_lists(arrived_ref, weights_hbm, weights, terms, sems)

        @pl.when(section_ref[0] == 1)
        def _():
            terms[...] = arrived_ref[...]

        sum_terms(key_ref, table_ref, terms, forcing)

    tiles = STRIDE // LANES
    base = step * tiles
    pieces = [
        forcing[pl.ds(pl.multiple_of((base + t) * 8, 8), 8), :] for t in range(tiles)
    ]
    fields = jnp.concatenate(pieces, 1)
    operand = jnp.concatenate([fields, fields], 0).astype(BF16)
    added = jnp.dot(write_ref[...], operand, preferred_element_type=F32)
    out_ref[:, :SPLIT] = (swept_ref[...].astype(F32) + added[:, :SPLIT]).astype(BF16)
    current = advance(ops_ref, (state_a, state_b), (coef_a, coef_b))
    out_ref[:, SPLIT:] = (current.astype(F32) + added[:, SPLIT:]).astype(BF16)


def late(section, key, table, arrived, weights, write, ops, swept, state, coef):
    levels, cells = state.shape
    lists, halves, cap, square = weights.shape
    slots, width = arrived.shape
    ratio = STRIDE // SPLIT
    whole = pl.BlockSpec(memory_space=pltpu.VMEM)
    second = pl.BlockSpec((levels, SPLIT), lambda i: (0, i * ratio + 1))
    third = pl.BlockSpec((levels, SPLIT), lambda i: (0, i * ratio + 2))
    return pl.pallas_call(
        late_kernel,
        grid=(cells // STRIDE,),
        out_shape=jax.ShapeDtypeStruct((levels, cells), BF16),
        in_specs=[
            pl.BlockSpec(memory_space=pltpu.SMEM),
            whole,
            whole,
            whole,
            pl.BlockSpec(memory_space=pl.ANY),
            whole,
            whole,
            pl.BlockSpec((levels, SPLIT), lambda i: (0, i)),
            second,
            third,
            second,
            third,
        ],
        out_specs=pl.BlockSpec((levels, STRIDE), lambda i: (0, i)),
        scratch_shapes=[
            pltpu.VMEM(weights.shape, BF16),
            pltpu.VMEM((slots, width), BF16),
            pltpu.VMEM((cells // LANES * 8, LANES), F32),
            pltpu.SemaphoreType.DMA((lists // GROUP,)),
        ],
        compiler_params=pltpu.CompilerParams(vmem_limit_bytes=VMEM_LIMIT),
        name="late",
    )(section, key, table, arrived, weights, write, ops, swept, state, state, coef, coef)


def body(
    adjoint_state,
    tangent_coef,
    column_ops,
    surf_read,
    surf_write,
    remap_weights,
    pair_atmos,
    pair_ocean,
    list_len,
    ocean_owned,
):
    section = lax.axis_index("sec")
    lists, cap = pair_atmos.shape[1:]
    blocks = ocean_owned.shape[1]
    pairs = blocks // 2
    state = adjoint_state[0]
    arrived_ids = lax.all_to_all(pair_ocean[0], "tile", split_axis=0, concat_axis=0, tiled=True)

    surface = surface_blocks(surf_read[0], state)
    partner = lax.ppermute(surface, "sec", [(0, 1), (1, 0)])

    live = lax.broadcasted_iota(jnp.int32, (lists, cap), 1) < list_len[0][:, None]
    atmos = pair_atmos[0]
    atmos_key = jnp.where(live, (atmos & 1) * pairs + (atmos >> 1), -1)
    keys = (lists * cap // LANES, LANES)
    atmos_key = atmos_key.reshape(keys).astype(F32)
    ocean_key = arrived_ids.reshape(keys).astype(F32)
    padded = -(-blocks // LANES) * LANES
    owned = jnp.pad(ocean_owned[0].reshape(pairs, 2).T.reshape(1, blocks), ((0, 0), (0, padded - blocks)), constant_values=-2)
    owned_table = owned.astype(F32)
    plain_table = lax.broadcasted_iota(jnp.int32, (1, padded), 1).astype(F32)
    first = section == 0
    out_key = jnp.where(first, ocean_key, atmos_key)
    in_key = jnp.where(first, atmos_key, ocean_key)
    out_table = jnp.where(first, owned_table, plain_table)
    in_table = jnp.where(first, plain_table, owned_table)
    which = section.reshape(1).astype(jnp.int32)

    weights = remap_weights[0].reshape(lists, cap // 8, 8, BLK * BLK)
    payload = outgoing(which, out_key, out_table, partner, weights)
    received = lax.all_to_all(
        payload.reshape(lists, cap, NF * BLK), "tile", split_axis=0, concat_axis=0, tiled=True
    )
    ops = column_ops[0].transpose(0, 2, 1)
    swept = early_sweep(ops, state, tangent_coef[0])
    write = surf_write[0]
    coarse = lax.reduce_precision(write, 8, 7)
    fine = write - coarse
    operand = jnp.concatenate([coarse, coarse, fine, fine], 1).astype(BF16)
    arrived = received.reshape(lists * cap, NF * BLK)
    out = late(
        which, in_key, in_table, arrived, weights, operand, ops, swept, state, tangent_coef[0]
    )
    return out[None]


def solution(mesh):
    in_specs = (
        P("sec", None, "tile"),
        P("sec", None, "tile"),
        P("sec", None, None, None),
        P("sec", None, None),
        P("sec", None, None),
        P("tile", None, None, None),
        P("tile", None, None),
        P("tile", None, None),
        P("tile", None),
        P("tile", None),
    )
    out_specs = P("sec", None, "tile")
    return jax.shard_map(body, mesh=mesh, in_specs=in_specs, out_specs=out_specs, check_vma=False)
```

time: 275 us -> 78.3 us (0.28)
  matrix products: 107 us -> 0 us
  local copies, waits for them, and re-layouts: 108 us -> 6.2 us
  Pallas kernels: 0 us -> 46.5 us
  other arithmetic: 17.5 us -> 2.06 us
  starting transfers between devices: 32.1 us -> 23.1 us
  waiting for transfers between devices: 7.11 us -> 0.01 us
    dot_general x22 -> x0, matrix products: 107 us -> none  [the longest x16 68.8 us: advance(): lax.dot_general(operator, current, (((0,), (0,)), ((), ())), preferred_el...]
    while x49 -> x0, local copies, waits for them, and re-layouts: 70.3 us -> none
    pallas_call x0 -> x4, Pallas kernels: none -> 46.5 us  [the longest x1 22.7 us: late(): pl.pallas_call(late_kernel, grid=(cells // STRIDE,), out_shape=jax.ShapeD...]
    unnamed x26 -> x17, local copies, waits for them, and re-layouts: 18.3 us -> 4.62 us
    scatter-add x2 -> x0, other arithmetic: 13.1 us -> none  [the longest x1 6.68 us: body(): jax.ops.segment_sum(arriving.reshape(slot_count, NF * BLK), position, num...]
    gather x3 -> x0, local copies, waits for them, and re-layouts: 8.31 us -> none  [the longest x2 4.37 us: body(): picked = surface_blocks[source]]
    all_to_all x3 -> x2, waiting for transfers between devices: 6.34 us -> 0.01 us  [the longest x1 0.01 us: body(): lax.all_to_all(pair_ocean[0], 'tile', split_axis=0, concat_axis=0, tiled=...]
    all_to_all x3 -> x2, starting transfers between devices: 26.6 us -> 22 us  [the longest x1 12 us: body(): lax.all_to_all(pair_ocean[0], 'tile', split_axis=0, concat_axis=0, tiled=...]
  transfers between devices with their start and end apart: 5 -> 3, of which waited for: 2 -> 0; matrix products, arithmetic and copies ran while one was open for 66% -> 7% of each run, Pallas kernels for 0% -> 20%
where the time goes in v2:
time: 78.3 us; the launch traced here: 78 us
  Pallas kernels  46.5 us (59%)
  starting transfers between devices  23.1 us (30%)
  local copies, waits for them, and re-layouts  6.2 us (8%)
  other arithmetic  2.06 us (3%)
    pallas_call x1, Pallas kernels, late(): pl.pallas_call(late_kernel, grid=(cells // STRIDE,), out_shape=jax.ShapeD...  22.7 us
    all_to_all x1, starting transfers between devices, body(): lax.all_to_all(pair_ocean[0], 'tile', split_axis=0, concat_axis=0, tiled=...  12 us
    pallas_call x1, Pallas kernels, early_sweep(): pl.pallas_call(early_kernel, grid=(steps,), out_shape=jax.ShapeDtypeStruc...  11.1 us
    all_to_all x1, starting transfers between devices, body(): lax.all_to_all(payload.reshape(lists, cap, NF * BLK), 'tile', split_axis=...  10.1 us
    pallas_call x1, Pallas kernels, outgoing(): pl.pallas_call(outgoing_kernel, out_shape=jax.ShapeDtypeStruct((slots, wi...  8.02 us
    pallas_call x1, Pallas kernels, surface_blocks(): pl.pallas_call(surface_kernel, out_shape=jax.ShapeDtypeStruct((blocks, NF...  4.65 us
    unnamed x17, local copies, waits for them, and re-layouts  4.62 us
  transfers between devices with their start and end apart: 3, of which 0 were waited for; matrix products, arithmetic and copies ran while one was open for 7% of the time, Pallas kernels for 20%

profile of v2, /device:TPU:1, one launch (start us, length us, event | category | flops | bytes accessed | tf_op | source)
XLA Modules:
  0.0 78.0 jit_solution(16632618209086534638)
XLA Ops:
  0.0 0.0 copy-start.4
  0.0 0.0 copy-start.3
  0.0 0.0 copy-start.6
  0.0 1.4 %copy.22 = s32[1,64,16]{2,1,0:T(8,128)} copy(s32[1,64,16]{1,2,0:T(8,128)} %param.17) | data formatting | bytes 8192 | tf_op args[7]
  1.4 12.0 %all-to-all-start = ((s32[64,1,16]{2,1,0:T(1,128)}), s32[64,1,16]{2,1,0:T(1,128)S(1)}, u32[]{:S(2)}, u32[]{:S(2)}) async-start(s32[64,1,16]{2,1,0:T(1,128)} %bitcast.1), calls=%async_computation | async-start | bytes 65536 | tf_op jit(solution)/shard_map/all_to_all | solution.py:413
  13.4 4.6 %surface.1 = bf16[576,256]{1,0:T(8,128)(2,1)} custom-call(bf16[4,75]{1,0:T(4,128)(2,1)} %bitcast.32, bf16[75,36864]{1,0:T(8,128)(2,1)} %bitcast.16), custom_call_target="tpu_custom_call" | custom-call | tf_op jit(solution)/shard_map/surface/pallas_call | solution.py:61
  18.1 0.0 copy-start.5
  18.1 0.0 copy-start.1
  18.1 1.0 %collective-permute-start = (bf16[576,256]{1,0:T(8,128)(2,1)}, bf16[576,256]{1,0:T(8,128)(2,1)S(1)}, u32[]{:S(2)}, u32[]{:S(2)}) collective-permute-start(bf16[576,256]{1,0:T(8,128)(2,1)} %surface.1), channel_id=1, source_target_pairs={{0,64},{64,0},{1,65},{65,1},{2,66},{66,2},{3,67},{67,3},{4,68},{68... | collective-permute-start | bytes 884744 | tf_op jit(solution)/shard_map/ppermute | solution.py:416
  19.1 0.0 copy-done.4
  19.1 0.0 copy-done.3
  19.2 0.1 reshape_squeeze.6
  19.3 0.1 copy.23
  19.4 0.1 reshape.41
  19.5 0.6 broadcast_select_fusion
  20.1 0.6 broadcast.27
  20.7 0.0 copy-done.6
  20.7 0.7 reduce.8
  21.4 0.1 lt.13
  21.5 0.1 iota.19
  21.6 0.1 copy.21
  21.6 0.1 add.10
  21.7 0.1 lt.14
  21.8 0.1 lt.15
  21.9 0.0 all-to-all-done
  21.9 0.1 convert_reduce_fusion
  22.0 0.1 convert_element_type.28
  22.1 0.6 convert_select_fusion
  22.7 0.0 collective-permute-done.blocks_ref
  22.7 0.0 copy-start.2
  22.7 0.7 copy-done.2
  23.4 8.0 %outgoing.1 = bf16[1024,256]{1,0:T(8,128)(2,1)} custom-call(s32[1]{0:T(128)} %bitcast.section_ref, f32[8,128]{1,0:T(8,128)} %get-tuple-element.5.key_ref, f32[1,640]{1,0:T(1,128)} %get-tuple-element.7.table_ref, bf16[576,256]{1,0:T(8,128)(2,1)} %copy-done.2, bf16[64,2,8,4096]{3,2,1,0:T(8,128)(2,1)} %bitcast.25), custom_call_target="tpu_custom_call" | custom-call | tf_op jit(solution)/shard_map/outgoing/pallas_call | solution.py:174
  31.4 10.1 %all-to-all-start.1 = ((bf16[64,16,256]{2,1,0:T(8,128)(2,1)}), bf16[64,16,256]{2,1,0:T(8,128)(2,1)S(1)}, u32[]{:S(2)}, u32[]{:S(2)}) async-start(bf16[64,16,256]{2,1,0:T(8,128)(2,1)} %bitcast.30), calls=%async_computation.1 | async-start | bytes 1048576 | tf_op jit(solution)/shard_map/all_to_all | solution.py:437
  41.5 0.0 copy-done.5
  41.5 0.7 copy.25.write_ref
  42.2 0.0 copy-done.1
  42.2 1.1 %copy.24 = bf16[1,16,75,75]{2,3,1,0:T(8,128)(2,1)} copy(bf16[1,16,75,75]{3,1,2,0:T(8,128)(2,1)S(1)} %copy-done.1) | data formatting | bytes 360000 | tf_op args[2]
  43.3 11.1 %early.1.swept_ref = bf16[75,12288]{1,0:T(8,128)(2,1)} custom-call(bf16[16,75,75]{2,1,0:T(8,128)(2,1)} %bitcast.27, bf16[75,36864]{1,0:T(8,128)(2,1)} %bitcast.17, bf16[75,36864]{1,0:T(8,128)(2,1)} %bitcast.18, bf16[75,36864]{1,0:T(8,128)(2,1)} %bitcast.21, bf16[75,36864]{1,0:T(8,128)(2,1)} %bitcast.22), custom_call_target="tpu_custom_call" | custom-call | tf_op jit(solution)/shard_map/early/pallas_call | solution.py:214
  54.4 0.0 all-to-all-done.1
  54.4 0.0 copy-start
  54.4 0.8 %copy-done = bf16[64,16,256]{2,1,0:T(8,128)(2,1)} copy-done((bf16[64,16,256]{2,1,0:T(8,128)(2,1)}, bf16[64,16,256]{2,1,0:T(8,128)(2,1)S(1)}, u32[]{:S(2)}) %copy-start) | copy-done | bytes 524312
  55.2 22.7 %late.1 = bf16[75,36864]{1,0:T(8,128)(2,1)} custom-call(s32[1]{0:T(128)} %bitcast.section_ref, f32[8,128]{1,0:T(8,128)} %get-tuple-element.6.key_ref, f32[1,640]{1,0:T(1,128)} %get-tuple-element.8.table_ref, bf16[1024,256]{1,0:T(8,128)(2,1)} %bitcast.29, bf16[64,2,8,4096]{3,2,1,0:T(8,128)(2,1)} %bitcast.26, bf16[75,16]{1,0:T(8,128)(2,1)} %copy.25.write_ref, ...), custom_call_target="tpu_custom_call" | custom-call | tf_op jit(solution)/shard_map/late/pallas_call | solution.py:366
  (5 shorter events, 0.0 us)
Async XLA Ops:
  0.0 19.1 %copy-start.4 = (s32[1,576]{1,0:T(1,128)S(1)}, s32[1,576]{1,0:T(1,128)}, u32[]{:S(2)}) copy-start(s32[1,576]{1,0:T(1,128)} %param.19) | copy-start | bytes 6916
  0.0 19.1 %copy-start.3 = (s32[1,64,16]{1,2,0:T(8,128)S(1)}, s32[1,64,16]{1,2,0:T(8,128)}, u32[]{:S(2)}) copy-start(s32[1,64,16]{1,2,0:T(8,128)} %param.16) | copy-start | bytes 12292
  0.0 20.7 %copy-start.6 = (s32[1,64]{1,0:T(1,128)S(1)}, s32[1,64]{1,0:T(1,128)}, u32[]{:S(2)}) copy-start(s32[1,64]{1,0:T(1,128)} %param.18) | copy-start | bytes 772
  1.4 20.4 %all-to-all-start = ((s32[64,1,16]{2,1,0:T(1,128)}), s32[64,1,16]{2,1,0:T(1,128)S(1)}, u32[]{:S(2)}, u32[]{:S(2)}) async-start(s32[64,1,16]{2,1,0:T(1,128)} %bitcast.1), calls=%async_computation | async-start | bytes 65536 | tf_op jit(solution)/shard_map/all_to_all | solution.py:413
  18.1 23.4 %copy-start.5 = (f32[1,75,4]{1,2,0:T(4,128)S(1)}, f32[1,75,4]{1,2,0:T(4,128)}, u32[]{:S(2)}) copy-start(f32[1,75,4]{1,2,0:T(4,128)} %param.14) | copy-start | bytes 3604
  18.1 24.2 %copy-start.1 = (bf16[1,16,75,75]{3,1,2,0:T(8,128)(2,1)S(1)}, bf16[1,16,75,75]{3,1,2,0:T(8,128)(2,1)}, u32[]{:S(2)}) copy-start(bf16[1,16,75,75]{3,1,2,0:T(8,128)(2,1)} %param.12) | copy-start | bytes 540004
  18.1 4.6 %collective-permute-start = (bf16[576,256]{1,0:T(8,128)(2,1)}, bf16[576,256]{1,0:T(8,128)(2,1)S(1)}, u32[]{:S(2)}, u32[]{:S(2)}) collective-permute-start(bf16[576,256]{1,0:T(8,128)(2,1)} %surface.1), channel_id=1, source_target_pairs={{0,64},{64,0},{1,65},{65,1},{2,66},{66,2},{3,67},{67,3},{4,68},{68... | collective-permute-start | bytes 884744 | tf_op jit(solution)/shard_map/ppermute | solution.py:416
  22.7 0.7 copy-start.2
  31.4 23.0 %all-to-all-start.1 = ((bf16[64,16,256]{2,1,0:T(8,128)(2,1)}), bf16[64,16,256]{2,1,0:T(8,128)(2,1)S(1)}, u32[]{:S(2)}, u32[]{:S(2)}) async-start(bf16[64,16,256]{2,1,0:T(8,128)(2,1)} %bitcast.30), calls=%async_computation.1 | async-start | bytes 1048576 | tf_op jit(solution)/shard_map/all_to_all | solution.py:437
  54.4 0.8 %copy-start = (bf16[64,16,256]{2,1,0:T(8,128)(2,1)}, bf16[64,16,256]{2,1,0:T(8,128)(2,1)S(1)}, u32[]{:S(2)}) copy-start(bf16[64,16,256]{2,1,0:T(8,128)(2,1)S(1)} %all-to-all-done.1) | copy-start | bytes 1572868

commit v3 on v2

v3 whole, which is shorter than its diff:
```python
import jax
import jax.numpy as jnp
from jax import lax
from jax.experimental import pallas as pl
from jax.experimental.pallas import tpu as pltpu
from jax.sharding import PartitionSpec as P

NF = 4
BLK = 64
NSTEP = 16
LANES = 128
GROUP = 8
WIDTH = 4096
FIRST = 2
SECOND = 4
BF16 = jnp.bfloat16
F32 = jnp.float32


def lanes_below(shape, edge):
    return lax.broadcasted_iota(jnp.int32, shape, len(shape) - 1) < edge


def advance(ops_ref, current, coef):
    factors = coef.astype(F32)
    for step in range(NSTEP):
        stepped = jnp.dot(ops_ref[step], current, preferred_element_type=F32)
        current = (stepped * factors).astype(BF16)
    return current


def early_column(block):
    return block // 2 * 3 + block % 2


def surface_kernel(
    read_ref, ops_ref, state_hbm, coef_hbm, out_ref, swept_hbm, state, coef, swept, held, sems
):
    parts = sems.shape[0] - 2
    tiles = WIDTH // LANES

    def columns(part):
        return pl.ds(pl.multiple_of(part * WIDTH, WIDTH), WIDTH)

    def fetch(part):
        return pltpu.make_async_copy(
            state_hbm.at[:, columns(part)], state.at[:, columns(part)], sems.at[part]
        )

    factors = pltpu.make_async_copy(coef_hbm.at[:, pl.ds(0, WIDTH)], coef, sems.at[parts])
    store = pltpu.make_async_copy(swept, swept_hbm.at[:, pl.ds(0, WIDTH)], sems.at[parts + 1])
    fetch(0).start()
    factors.start()
    for part in range(1, parts):
        fetch(part).start()

    def compute(part):
        fields = jnp.dot(read_ref[...], state[:, columns(part)], preferred_element_type=F32)
        for tile in range(tiles):
            row = pl.multiple_of((part * tiles + tile) * 8, 8)
            held[pl.ds(row, NF), :] = fields[:, tile * LANES : (tile + 1) * LANES]

    fetch(0).wait()
    factors.wait()
    swept[...] = advance(ops_ref, state[:, :WIDTH], coef[...])
    store.start()
    compute(0)

    def following(part, carry):
        fetch(part).wait()
        compute(part)
        return carry

    lax.fori_loop(1, parts, following, 0)
    pairs = out_ref.shape[0] // 2
    left = lanes_below((pairs, LANES), BLK)
    for duo in range(NF // 2):
        first = held[pl.ds(2 * duo, pairs, stride=8), :]
        second = held[pl.ds(2 * duo + 1, pairs, stride=8), :]
        cols = slice(duo * LANES, (duo + 1) * LANES)
        even = jnp.where(left, first, pltpu.roll(second, BLK, 1))
        odd = jnp.where(left, pltpu.roll(first, BLK, 1), second)
        out_ref[:pairs, cols] = even.astype(BF16)
        out_ref[pairs:, cols] = odd.astype(BF16)
    store.wait()


def surface_blocks(read, ops, state, coef):
    levels, cells = state.shape
    blocks = cells // BLK
    parts = cells // WIDTH
    whole = pl.BlockSpec(memory_space=pltpu.VMEM)
    there = pl.BlockSpec(memory_space=pl.ANY)
    return pl.pallas_call(
        surface_kernel,
        out_shape=(
            jax.ShapeDtypeStruct((blocks, NF * BLK), BF16),
            pltpu.HBM((levels, cells // 3 * 2), BF16),
        ),
        in_specs=[whole, whole, there, there],
        out_specs=(whole, there),
        scratch_shapes=[
            pltpu.VMEM((levels, cells), BF16),
            pltpu.VMEM((levels, WIDTH), BF16),
            pltpu.VMEM((levels, WIDTH), BF16),
            pltpu.VMEM((blocks // 2 * 8, LANES), F32),
            pltpu.SemaphoreType.DMA((parts + 2,)),
        ],
        compiler_params=pltpu.CompilerParams(vmem_limit_bytes=24 << 20),
        name="surface",
    )(read, ops, state, coef)


def fetch_weights(weights_hbm, weights, sems, part):
    lists = pl.ds(part * GROUP, GROUP)
    return pltpu.make_async_copy(weights_hbm.at[lists], weights.at[lists], sems.at[part])


def half_list(weights, tile, half):
    return jnp.concatenate(
        [weights[tile, half, :, q * LANES : (q + 1) * LANES] for q in range(BLK // 2)], 0
    )


def pick(values, lanes):
    return jnp.take_along_axis(values, lanes, axis=1, mode="promise_in_bounds")


def widened(values):
    rows, cols = values.shape
    return jnp.concatenate([values, jnp.zeros((rows, LANES - cols), values.dtype)], 1)


def slot_rows(values):
    lists = values.shape[0]
    lane = lax.broadcasted_iota(jnp.int32, (lists, LANES), 1)
    row = lax.broadcasted_iota(jnp.int32, (lists, LANES), 0)
    spread = jnp.where((lane >> 4) == (row & 7), pick(widened(values), lane & 15), 0.0)
    return jnp.sum(spread.reshape(lists // 8, 8, LANES), 1)


def even_first(values, padded):
    count = values.shape[1]
    pairs = count // 2
    lane = lax.broadcasted_iota(jnp.int32, (8, LANES), 1)
    sources = []
    for start in range(0, count, LANES):
        source = values[:, start : min(start + LANES, count)]
        sources.append(source if source.shape[1] == LANES else widened(source))
    sources = [jnp.broadcast_to(source, (8, LANES)) for source in sources]
    tiles = []
    for tile in range(padded // LANES):
        spots = [
            2 * j if j < pairs else 2 * (j - pairs) + 1
            for j in range(tile * LANES, min((tile + 1) * LANES, count))
        ]
        at = tile * LANES + lane
        wanted = jnp.where(at < pairs, 2 * at, 2 * (at - pairs) + 1)
        result = jnp.full((8, LANES), -2.0, F32)
        for index in sorted({spot // LANES for spot in spots}):
            inside = ((wanted >> 7) == index) & (at < count)
            result = jnp.where(inside, pick(sources[index], wanted & 127), result)
        tiles.append(result)
    return jnp.concatenate(tiles, 1)[:1]


def outgoing_kernel(
    section_ref,
    atmos_ref,
    length_ref,
    ids_ref,
    owned_ref,
    blocks_ref,
    ops_ref,
    weights_hbm,
    state_hbm,
    coef_hbm,
    swept_in,
    out_ref,
    in_key_ref,
    in_table_ref,
    swept_hbm,
    chosen,
    weights,
    state,
    coef,
    swept,
    weight_sems,
    sems,
):
    count = state.shape[0]

    def fetch(block):
        columns = pl.ds(pl.multiple_of(early_column(FIRST + block) * WIDTH, WIDTH), WIDTH)
        return (
            pltpu.make_async_copy(state_hbm.at[:, columns], state.at[block], sems.at[0, block]),
            pltpu.make_async_copy(coef_hbm.at[:, columns], coef.at[block], sems.at[1, block]),
        )

    def store(block):
        columns = pl.ds(pl.multiple_of((FIRST + block) * WIDTH, WIDTH), WIDTH)
        return pltpu.make_async_copy(
            swept.at[block], swept_hbm.at[:, columns], sems.at[2, block]
        )

    for block in range(count):
        for copy in fetch(block):
            copy.start()

    @pl.when(section_ref[0] == 1)
    def _():
        for part in range(weight_sems.shape[0]):
            fetch_weights(weights_hbm, weights, weight_sems, part).start()

    def sweep_block(block, carry):
        for copy in fetch(block):
            copy.wait()
        swept[block] = advance(ops_ref, state[block], coef[block])
        store(block).start()
        return carry

    lax.fori_loop(0, count, sweep_block, 0)
    blocks = blocks_ref.shape[0]
    pairs = blocks // 2
    padded = in_table_ref.shape[1]
    parts = in_key_ref.shape[0]
    first = section_ref[0] == 0
    lane = lax.broadcasted_iota(jnp.int32, (8, LANES), 1)
    row = lax.broadcasted_iota(jnp.int32, (8, LANES), 0)
    lengths = jnp.broadcast_to(widened(length_ref[...].astype(F32)), (8, LANES))
    live = (lane & 15).astype(F32) < pick(lengths, row * 8 + (lane >> 4))
    atmos = atmos_ref[...]
    atmos = ((atmos & 1) * pairs + (atmos >> 1)).astype(F32)
    atmos_key = jnp.where(live, slot_rows(widened(atmos).T[: atmos.shape[1]]), -1.0)
    ocean_key = slot_rows(ids_ref[:, 0, :].astype(F32))
    owned_table = even_first(owned_ref[...].astype(F32), padded)
    plain_table = lax.broadcasted_iota(jnp.int32, (1, padded), 1).astype(F32)
    out_key = jnp.where(first, ocean_key, atmos_key)
    out_table = jnp.where(first, owned_table, plain_table)
    in_key_ref[...] = jnp.where(first, atmos_key, ocean_key)
    in_table_ref[...] = jnp.where(first, plain_table, owned_table)

    for part in range(parts):
        key = jnp.broadcast_to(out_key[part : part + 1, :], (LANES, LANES)).T
        pieces = []
        for start in range(0, blocks, LANES):
            stop = min(start + LANES, blocks)
            piece = jnp.where(key == out_table[:, start : start + LANES], 1.0, 0.0).astype(BF16)
            pieces.append(piece[:, : stop - start])
        chosen[part * LANES : (part + 1) * LANES, :] = jnp.dot(
            jnp.concatenate(pieces, 1), blocks_ref[...], preferred_element_type=F32
        )

    @pl.when(first)
    def _():
        out_ref[...] = chosen[...].astype(BF16)

    @pl.when(jnp.logical_not(first))
    def _():
        own = (lane & 7) == row
        left = lane < BLK

        def lists(part, carry):
            fetch_weights(weights_hbm, weights, weight_sems, part).wait()
            for inner in range(GROUP):
                tile = part * GROUP + inner
                rows = pl.ds(pl.multiple_of(tile * 16, 16), 16)
                values = chosen[rows, :]
                results = []
                for half in range(2):
                    lines = []
                    for field in range(NF):
                        duo = values[
                            half * 8 : half * 8 + 8, field // 2 * LANES : (field // 2 + 1) * LANES
                        ]
                        for parity in range(2):
                            line = []
                            for side in range(2):
                                source = (field % 2) * BLK + 2 * (side * 16 + (lane >> 3)) + parity
                                line.append(jnp.where(own, pick(duo, source), 0.0))
                            lines.append(jnp.concatenate(line, 1))
                    product = jnp.dot(
                        jnp.concatenate(lines, 0).astype(BF16),
                        half_list(weights, tile, half),
                        preferred_element_type=F32,
                    )
                    sums = []
                    for field in range(NF):
                        even = product[field * 16 : field * 16 + 8]
                        odd = product[field * 16 + 8 : field * 16 + 16]
                        total = jnp.where(left, even, odd)
                        sums.append(total + pltpu.roll(total, BLK, 1))
                    results.append(
                        [jnp.where(left, sums[2 * duo], sums[2 * duo + 1]) for duo in range(NF // 2)]
                    )
                for duo in range(NF // 2):
                    out_ref[rows, duo * LANES : (duo + 1) * LANES] = jnp.concatenate(
                        [results[0][duo], results[1][duo]], 0
                    ).astype(BF16)
            return carry

        lax.fori_loop(0, parts, lists, 0)

    for block in range(count):
        store(block).wait()


def outgoing(section, atmos, length, ids, owned, blocks, ops, weights, state, coef, swept):
    lists, halves, cap, square = weights.shape
    slots = lists * halves * cap
    count, width = blocks.shape
    padded = -(-count // LANES) * LANES
    levels = state.shape[0]
    whole = pl.BlockSpec(memory_space=pltpu.VMEM)
    there = pl.BlockSpec(memory_space=pl.ANY)
    held = pltpu.VMEM((SECOND - FIRST, levels, WIDTH), BF16)
    return pl.pallas_call(
        outgoing_kernel,
        out_shape=(
            jax.ShapeDtypeStruct((slots, width), BF16),
            jax.ShapeDtypeStruct((slots // LANES, LANES), F32),
            jax.ShapeDtypeStruct((1, padded), F32),
            pltpu.HBM(swept.shape, BF16),
        ),
        in_specs=[pl.BlockSpec(memory_space=pltpu.SMEM)] + [whole] * 6 + [there] * 4,
        out_specs=(whole, whole, whole, there),
        input_output_aliases={10: 3},
        scratch_shapes=[
            pltpu.VMEM((slots, width), F32),
            pltpu.VMEM(weights.shape, BF16),
            held,
            held,
            held,
            pltpu.SemaphoreType.DMA((lists // GROUP,)),
            pltpu.SemaphoreType.DMA((3, SECOND - FIRST)),
        ],
        compiler_params=pltpu.CompilerParams(vmem_limit_bytes=32 << 20),
        name="outgoing",
    )(section, atmos, length, ids, owned, blocks, ops, weights, state, coef, swept)


def early_kernel(ops_ref, state_ref, coef_ref, swept_hbm, out_ref):
    out_ref[...] = advance(ops_ref, state_ref[...], coef_ref[...])


def early_sweep(ops, state, coef, swept, start, stop):
    levels, cells = state.shape
    columns = pl.BlockSpec((levels, WIDTH), lambda i: (0, early_column(i + start)))
    there = pl.BlockSpec(memory_space=pl.ANY)
    return pl.pallas_call(
        early_kernel,
        grid=(stop - start,),
        out_shape=pltpu.HBM(swept.shape, BF16),
        in_specs=[pl.BlockSpec(ops.shape, lambda i: (0, 0, 0)), columns, columns, there],
        out_specs=pl.BlockSpec((levels, WIDTH), lambda i: (0, i + start)),
        input_output_aliases={3: 0},
        compiler_params=pltpu.CompilerParams(vmem_limit_bytes=16 << 20),
        name="early",
    )(ops, state, coef, swept)


def backward_lists(arrived_ref, weights_hbm, weights, terms, weight_sems):
    lane = lax.broadcasted_iota(jnp.int32, (8, LANES), 1)
    row = lax.broadcasted_iota(jnp.int32, (8, LANES), 0)
    left = lane < BLK
    source = (((lane >> 1) & 15) << 3) + row
    half_kind = ((lane >> 5) & 1) * 2 + (lane & 1)

    def lists(part, carry):
        fetch_weights(weights_hbm, weights, weight_sems, part).wait()
        for inner in range(GROUP):
            tile = part * GROUP + inner
            rows = pl.ds(pl.multiple_of(tile * 16, 16), 16)
            echoes = arrived_ref[rows, :].astype(F32)
            results = []
            for half in range(2):
                lines = []
                for duo in range(NF // 2):
                    both = echoes[half * 8 : half * 8 + 8, duo * LANES : (duo + 1) * LANES]
                    turned = pltpu.roll(both, BLK, 1)
                    lines += [
                        jnp.where(left, both, 0.0),
                        jnp.where(left, 0.0, turned),
                        jnp.where(left, turned, 0.0),
                        jnp.where(left, 0.0, both),
                    ]
                product = lax.dot_general(
                    jnp.concatenate(lines, 0).astype(BF16),
                    half_list(weights, tile, half),
                    (((1,), (1,)), ((), ())),
                    preferred_element_type=F32,
                )
                outs = []
                for duo in range(NF // 2):
                    fields = []
                    for field in (2 * duo, 2 * duo + 1):
                        total = None
                        for side in range(2):
                            for parity in range(2):
                                start = field * 16 + parity * 8
                                value = pick(
                                    product[start : start + 8, side * LANES : (side + 1) * LANES],
                                    source,
                                )
                                kind = side * 2 + parity
                                total = (
                                    value
                                    if total is None
                                    else jnp.where(half_kind == kind, value, total)
                                )
                        fields.append(total)
                    outs.append(jnp.where(left, fields[0], fields[1]))
                results.append(outs)
            for duo in range(NF // 2):
                terms[rows, duo * LANES : (duo + 1) * LANES] = jnp.concatenate(
                    [results[0][duo], results[1][duo]], 0
                ).astype(BF16)
        return carry

    lax.fori_loop(0, weights.shape[0] // GROUP, lists, 0)


def sum_terms(key_ref, table_ref, terms, forcing):
    slots = terms.shape[0]
    pairs = forcing.shape[0] // 8
    table = jnp.broadcast_to(table_ref[...], (LANES, table_ref.shape[1])).T[: 2 * pairs]
    picks = [
        jnp.where(table == key_ref[r : r + 1, :], 1.0, 0.0).astype(BF16)
        for r in range(slots // LANES)
    ]
    total = jnp.dot(jnp.concatenate(picks, 1), terms[...], preferred_element_type=F32)
    left = lanes_below((pairs, LANES), BLK)
    for duo in range(NF // 2):
        even = total[:pairs, duo * LANES : (duo + 1) * LANES]
        odd = total[pairs:, duo * LANES : (duo + 1) * LANES]
        fields = (
            jnp.where(left, even, pltpu.roll(odd, BLK, 1)),
            jnp.where(left, pltpu.roll(even, BLK, 1), odd),
        )
        for n, field in enumerate(fields):
            coarse = field.astype(BF16).astype(F32)
            forcing[pl.ds(2 * duo + n, pairs, stride=8), :] = coarse
            forcing[pl.ds(NF + 2 * duo + n, pairs, stride=8), :] = field - coarse


def late_kernel(
    section_ref,
    key_ref,
    table_ref,
    arrived_ref,
    weights_hbm,
    write_ref,
    ops_ref,
    swept_ref,
    state_ref,
    coef_ref,
    out_hbm,
    terms,
    forcing,
    early,
    last,
    weights,
    weight_sems,
    sems,
):
    step = pl.program_id(0)
    backward = jnp.logical_and(step == 0, section_ref[0] == 0)

    @pl.when(backward)
    def _():
        for part in range(weight_sems.shape[0]):
            fetch_weights(weights_hbm, weights, weight_sems, part).start()

    slot = step % 2
    span = 3 * WIDTH
    ready = pltpu.make_async_copy(
        early.at[slot],
        out_hbm.at[:, pl.ds(pl.multiple_of(step * span, span), 2 * WIDTH)],
        sems.at[slot],
    )
    swept = pltpu.make_async_copy(
        last.at[slot],
        out_hbm.at[:, pl.ds(pl.multiple_of(step * span + 2 * WIDTH, WIDTH), WIDTH)],
        sems.at[2 + slot],
    )
    before = 1 - slot
    ready_before = pltpu.make_async_copy(
        early.at[before], out_hbm.at[:, pl.ds(0, 2 * WIDTH)], sems.at[before]
    )
    swept_before = pltpu.make_async_copy(
        last.at[before], out_hbm.at[:, pl.ds(0, WIDTH)], sems.at[2 + before]
    )

    last[slot] = advance(ops_ref, state_ref[...], coef_ref[...])

    @pl.when(backward)
    def _():
        backward_lists(arrived_ref, weights_hbm, weights, terms, weight_sems)

    @pl.when(step == 0)
    def _():
        @pl.when(section_ref[0] == 1)
        def _():
            terms[...] = arrived_ref[...]

        sum_terms(key_ref, table_ref, terms, forcing)

    write = write_ref[...]
    coarse = write.astype(BF16).astype(F32)
    fine = write - coarse
    factor = jnp.concatenate([coarse, coarse, fine, fine], 0).astype(BF16)

    def added(start, width):
        base = step * (span // LANES) + start // LANES
        fields = jnp.concatenate(
            [
                forcing[pl.ds(pl.multiple_of((base + t) * 8, 8), 8), :]
                for t in range(width // LANES)
            ],
            1,
        )
        operand = jnp.concatenate([fields, fields], 0).astype(BF16)
        return lax.dot_general(
            factor, operand, (((0,), (0,)), ((), ())), preferred_element_type=F32
        )

    early[slot] = (swept_ref[...].astype(F32) + added(0, 2 * WIDTH)).astype(BF16)
    ready.start()
    last[slot] = (last[slot].astype(F32) + added(2 * WIDTH, WIDTH)).astype(BF16)
    swept.start()

    @pl.when(step > 0)
    def _():
        ready_before.wait()
        swept_before.wait()

    @pl.when(step == pl.num_programs(0) - 1)
    def _():
        ready.wait()
        swept.wait()


def late(section, key, table, arrived, weights, write, ops, swept, state, coef):
    levels, cells = state.shape
    slots, width = arrived.shape
    whole = pl.BlockSpec(memory_space=pltpu.VMEM)
    columns = pl.BlockSpec((levels, WIDTH), lambda i: (0, 3 * i + 2))
    return pl.pallas_call(
        late_kernel,
        grid=(cells // (3 * WIDTH),),
        out_shape=jax.ShapeDtypeStruct((levels, cells), BF16),
        in_specs=[
            pl.BlockSpec(memory_space=pltpu.SMEM),
            whole,
            whole,
            whole,
            pl.BlockSpec(memory_space=pl.ANY),
            whole,
            whole,
            pl.BlockSpec((levels, 2 * WIDTH), lambda i: (0, i)),
            columns,
            columns,
        ],
        out_specs=pl.BlockSpec(memory_space=pl.ANY),
        scratch_shapes=[
            pltpu.VMEM((slots, width), BF16),
            pltpu.VMEM((cells // LANES * 8, LANES), F32),
            pltpu.VMEM((2, levels, 2 * WIDTH), BF16),
            pltpu.VMEM((2, levels, WIDTH), BF16),
            pltpu.VMEM(weights.shape, BF16),
            pltpu.SemaphoreType.DMA((weights.shape[0] // GROUP,)),
            pltpu.SemaphoreType.DMA((4,)),
        ],
        compiler_params=pltpu.CompilerParams(vmem_limit_bytes=36 << 20),
        name="late",
    )(section, key, table, arrived, weights, write, ops, swept, state, coef)


def body(
    adjoint_state,
    tangent_coef,
    column_ops,
    surf_read,
    surf_write,
    remap_weights,
    pair_atmos,
    pair_ocean,
    list_len,
    ocean_owned,
):
    section = lax.axis_index("sec")
    lists, cap = pair_atmos.shape[1:]
    state = pltpu.with_memory_space_constraint(adjoint_state[0], pltpu.HBM)
    coef = pltpu.with_memory_space_constraint(tangent_coef[0], pltpu.HBM)
    weights = pltpu.with_memory_space_constraint(
        remap_weights[0].reshape(lists, cap // 8, 8, BLK * BLK), pltpu.HBM
    )
    ops = column_ops[0].transpose(0, 2, 1)
    which = section.reshape(1).astype(jnp.int32)
    arrived_ids = lax.all_to_all(pair_ocean[0], "tile", split_axis=0, concat_axis=0, tiled=True)
    surface, swept = surface_blocks(surf_read[0], ops, state, coef)
    partner = lax.ppermute(surface, "sec", [(0, 1), (1, 0)])
    swept = early_sweep(ops, state, coef, swept, 1, FIRST)
    payload, in_key, in_table, swept = outgoing(
        which,
        pair_atmos[0].T,
        list_len,
        arrived_ids.reshape(lists, 1, cap),
        ocean_owned,
        partner,
        ops,
        weights,
        state,
        coef,
        swept,
    )
    received = lax.all_to_all(
        payload.reshape(lists, cap, NF * BLK), "tile", split_axis=0, concat_axis=0, tiled=True
    )
    swept = early_sweep(ops, state, coef, swept, SECOND, 6)
    swept = pltpu.with_memory_space_constraint(swept, pltpu.HBM)
    arrived = received.reshape(lists * cap, NF * BLK)
    write = surf_write[0].T
    out = late(which, in_key, in_table, arrived, weights, write, ops, swept, state, coef)
    return out[None]


def solution(mesh):
    in_specs = (
        P("sec", None, "tile"),
        P("sec", None, "tile"),
        P("sec", None, None, None),
        P("sec", None, None),
        P("sec", None, None),
        P("tile", None, None, None),
        P("tile", None, None),
        P("tile", None, None),
        P("tile", None),
        P("tile", None),
    )
    out_specs = P("sec", None, "tile")
    return jax.shard_map(body, mesh=mesh, in_specs=in_specs, out_specs=out_specs, check_vma=False)
```

time: 78.3 us -> 77.8 us (level)
  waiting for transfers between devices: 0.01 us -> 6.08 us
  starting transfers between devices: 23.1 us -> 19.2 us
  local copies, waits for them, and re-layouts: 6.2 us -> 2.75 us
  Pallas kernels: 46.5 us -> 49.2 us
  other arithmetic: 2.06 us -> 0 us
    all_to_all x1, starting transfers between devices: 10.1 us -> 6.54 us  [body(): lax.all_to_all(payload.reshape(lists, cap, NF * BLK), 'tile', split_axis=...]
    all_to_all x1, waiting for transfers between devices: 0.01 us -> 3.26 us  [body(): lax.all_to_all(pair_ocean[0], 'tile', split_axis=0, concat_axis=0, tiled=...]
    all_to_all x1, waiting for transfers between devices: 0.01 us -> 2.82 us  [body(): lax.all_to_all(payload.reshape(lists, cap, NF * BLK), 'tile', split_axis=...]
    pallas_call x4 -> x5, Pallas kernels: 46.5 us -> 49.2 us  [the longest x1 15.5 us: outgoing(): pl.pallas_call(outgoing_kernel, out_shape=(jax.ShapeDtypeStruct((slots, w...]
    unnamed x17 -> x14, local copies, waits for them, and re-layouts: 4.62 us -> 2.75 us
    select_n x2 -> x0, other arithmetic: 1.23 us -> none  [the longest x1 0.63 us: body(): out_table = jnp.where(first, owned_table, plain_table)]
  transfers between devices with their start and end apart: 3 -> 3, of which waited for: 0 -> 2; matrix products, arithmetic and copies ran while one was open for 7% -> 1% of each run, Pallas kernels for 20% -> 17%
where the time goes in v3:
time: 77.8 us; the launch traced here: 77.5 us
  Pallas kernels  49.2 us (63%)
  starting transfers between devices  19.2 us (25%)
  waiting for transfers between devices  6.08 us (8%)
  local copies, waits for them, and re-layouts  2.75 us (4%)
    pallas_call x1, Pallas kernels, outgoing(): pl.pallas_call(outgoing_kernel, out_shape=(jax.ShapeDtypeStruct((slots, w...  15.5 us
    pallas_call x1, Pallas kernels, late(): pl.pallas_call(late_kernel, grid=(cells // (3 * WIDTH),), out_shape=jax.S...  14.4 us
    pallas_call x2, Pallas kernels, early_sweep(): pl.pallas_call(early_kernel, grid=(stop - start,), out_shape=pltpu.HBM(sw...  13 us
    all_to_all x1, starting transfers between devices, body(): lax.all_to_all(pair_ocean[0], 'tile', split_axis=0, concat_axis=0, tiled=...  11.2 us
    all_to_all x1, starting transfers between devices, body(): lax.all_to_all(payload.reshape(lists, cap, NF * BLK), 'tile', split_axis=...  6.54 us
    pallas_call x1, Pallas kernels, surface_blocks(): pl.pallas_call(surface_kernel, out_shape=(jax.ShapeDtypeStruct((blocks, N...  6.23 us
    all_to_all x1, waiting for transfers between devices, body(): lax.all_to_all(pair_ocean[0], 'tile', split_axis=0, concat_axis=0, tiled=...  3.26 us
    all_to_all x1, waiting for transfers between devices, body(): lax.all_to_all(payload.reshape(lists, cap, NF * BLK), 'tile', split_axis=...  2.82 us
  transfers between devices with their start and end apart: 3, of which 2 were waited for; matrix products, arithmetic and copies ran while one was open for 1% of the time, Pallas kernels for 17%

profile of v3, /device:TPU:1, one launch (start us, length us, event | category | flops | bytes accessed | tf_op | source)
XLA Modules:
  0.0 77.5 jit_solution(38245289203246205)
XLA Ops:
  0.0 1.3 %copy.15 = bf16[1,16,75,75]{2,3,1,0:T(8,128)(2,1)S(1)} copy(bf16[1,16,75,75]{3,1,2,0:T(8,128)(2,1)} %param.12) | data formatting | bytes 360000 | tf_op args[2]
  1.3 0.0 copy-start.3
  1.3 0.7 copy-done.3
  2.0 0.0 copy-start.5
  2.0 6.2 %surface.1 = (bf16[576,256]{1,0:T(8,128)(2,1)S(1)}, bf16[75,24576]{1,0:T(8,128)(2,1)}) custom-call(bf16[4,75]{1,0:T(4,128)(2,1)S(1)} %bitcast.26, bf16[16,75,75]{2,1,0:T(8,128)(2,1)S(1)} %bitcast.18, bf16[75,36864]{1,0:T(8,128)(2,1)} %bitcast.27, bf16[75,36864]{1,0:T(8,128)(2,1)} %bitcast.32), custom_call_target="tpu_custom_call" | custom-call | tf_op jit(solution)/shard_map/surface/pallas_call | solution.py:94
  8.3 1.5 %collective-permute-start = (bf16[576,256]{1,0:T(8,128)(2,1)S(1)}, bf16[576,256]{1,0:T(8,128)(2,1)S(1)}, u32[]{:S(2)}, u32[]{:S(2)}) collective-permute-start(bf16[576,256]{1,0:T(8,128)(2,1)S(1)} %get-tuple-element.11), channel_id=1, source_target_pairs={{0,64},{64,0},{1,65},{65,1},{2,66},{66,2},{3,67},{67,3},{4,68},{68... | collective-permute-start | bytes 884744 | tf_op jit(solution)/shard_map/ppermute | solution.py:602
  9.7 0.0 copy-done.5
  9.7 0.7 copy.14
  10.4 11.2 %all-to-all-start = ((s32[64,1,16]{2,1,0:T(1,128)}), s32[64,1,16]{2,1,0:T(1,128)S(1)}, u32[]{:S(2)}, u32[]{:S(2)}) async-start(s32[64,1,16]{2,1,0:T(1,128)} %bitcast.3), calls=%async_computation | async-start | bytes 65536 | tf_op jit(solution)/shard_map/all_to_all | solution.py:600
  21.7 0.0 copy-start
  21.7 0.0 copy-start.1
  21.7 0.0 copy-start.4
  21.7 5.1 %early.2.swept_in = bf16[75,24576]{1,0:T(8,128)(2,1)} custom-call(bf16[16,75,75]{2,1,0:T(8,128)(2,1)S(1)} %bitcast.19, bf16[75,36864]{1,0:T(8,128)(2,1)} %bitcast.28, bf16[75,36864]{1,0:T(8,128)(2,1)} %bitcast.33, bf16[75,24576]{1,0:T(8,128)(2,1)} %get-tuple-element.12.swept_hbm), custom_call_target="tpu_custom_call", output_to_operand_aliasing={{}: (3, {})} | custom-call | tf_op jit(solution)/shard_map/early/pallas_call | solution.py:350
  26.8 3.3 %all-to-all-done.ids_ref = s32[64,1,16]{2,1,0:T(1,128)S(1)} async-done(((s32[64,1,16]{2,1,0:T(1,128)}), s32[64,1,16]{2,1,0:T(1,128)S(1)}, u32[]{:S(2)}, u32[]{:S(2)}) %all-to-all-start) | async-done | bytes 4128 | tf_op jit(solution)/shard_map/all_to_all | solution.py:600
  30.0 0.0 collective-permute-done.blocks_ref
  30.0 0.0 copy-done
  30.0 0.0 copy-done.1
  30.0 0.0 copy-done.4
  30.1 15.5 %outgoing.1 = (bf16[1024,256]{1,0:T(8,128)(2,1)}, f32[8,128]{1,0:T(8,128)S(1)}, f32[1,640]{1,0:T(1,128)S(1)}, bf16[75,24576]{1,0:T(8,128)(2,1)}) custom-call(s32[1]{0:T(128)} %bitcast.section_ref, s32[16,64]{1,0:T(8,128)S(1)} %bitcast.24, s32[1,64]{1,0:T(1,128)S(1)} %copy-done.4, ...), custom_call_target="tpu_custom_call", output_to_operand_aliasing={{3}: (10, {})} | custom-call | tf_op jit(solution)/shard_map/outgoing/pallas_call | solution.py:317
  45.6 6.5 %all-to-all-start.1 = ((bf16[64,16,256]{2,1,0:T(8,128)(2,1)}), bf16[64,16,256]{2,1,0:T(8,128)(2,1)S(1)}, u32[]{:S(2)}, u32[]{:S(2)}) async-start(bf16[64,16,256]{2,1,0:T(8,128)(2,1)} %bitcast.11), calls=%async_computation.1 | async-start | bytes 1048576 | tf_op jit(solution)/shard_map/all_to_all | solution.py:617
  52.1 0.0 copy-start.2
  52.2 8.0 %early.3.swept_ref = bf16[75,24576]{1,0:T(8,128)(2,1)} custom-call(bf16[16,75,75]{2,1,0:T(8,128)(2,1)S(1)} %bitcast.21, bf16[75,36864]{1,0:T(8,128)(2,1)} %bitcast.30, bf16[75,36864]{1,0:T(8,128)(2,1)} %bitcast.35, bf16[75,24576]{1,0:T(8,128)(2,1)} %get-tuple-element.16.swept_hbm), custom_call_target="tpu_custom_call", output_to_operand_aliasing={{}: (3, {})} | custom-call | tf_op jit(solution)/shard_map/early/pallas_call | solution.py:350
  60.1 2.8 %all-to-all-done.1 = bf16[64,16,256]{2,1,0:T(8,128)(2,1)S(1)} async-done(((bf16[64,16,256]{2,1,0:T(8,128)(2,1)}), bf16[64,16,256]{2,1,0:T(8,128)(2,1)S(1)}, u32[]{:S(2)}, u32[]{:S(2)}) %all-to-all-start.1) | async-done | bytes 524320 | tf_op jit(solution)/shard_map/all_to_all | solution.py:617
  63.0 0.0 copy-done.2
  63.0 14.4 %late.1 = bf16[75,36864]{1,0:T(8,128)(2,1)} custom-call(s32[1]{0:T(128)} %bitcast.section_ref, f32[8,128]{1,0:T(8,128)S(1)} %get-tuple-element.13.key_ref, f32[1,640]{1,0:T(1,128)S(1)} %get-tuple-element.14.table_ref, bf16[1024,256]{1,0:T(8,128)(2,1)S(1)} %bitcast.23, bf16[64,2,8,4096]{3,2,1,0:T(8,128)(2,1)} %bitcast.38, f32[4,75]{1,0:T(4,128)S(1)} %bitcast.25, ...), custom_call_target="tpu_custom_call" | custom-call | tf_op jit(solution)/shard_map/late/pallas_call | solution.py:548
Async XLA Ops:
  1.3 0.7 copy-start.3
  2.0 7.7 %copy-start.5 = (s32[1,64,16]{1,2,0:T(8,128)S(1)}, s32[1,64,16]{1,2,0:T(8,128)}, u32[]{:S(2)}) copy-start(s32[1,64,16]{1,2,0:T(8,128)} %param.17) | copy-start | bytes 12292
  8.3 21.8 %collective-permute-start = (bf16[576,256]{1,0:T(8,128)(2,1)S(1)}, bf16[576,256]{1,0:T(8,128)(2,1)S(1)}, u32[]{:S(2)}, u32[]{:S(2)}) collective-permute-start(bf16[576,256]{1,0:T(8,128)(2,1)S(1)} %get-tuple-element.11), channel_id=1, source_target_pairs={{0,64},{64,0},{1,65},{65,1},{2,66},{66,2},{3,67},{67,3},{4,68},{68... | collective-permute-start | bytes 884744 | tf_op jit(solution)/shard_map/ppermute | solution.py:602
  10.4 19.6 %all-to-all-start = ((s32[64,1,16]{2,1,0:T(1,128)}), s32[64,1,16]{2,1,0:T(1,128)S(1)}, u32[]{:S(2)}, u32[]{:S(2)}) async-start(s32[64,1,16]{2,1,0:T(1,128)} %bitcast.3), calls=%async_computation | async-start | bytes 65536 | tf_op jit(solution)/shard_map/all_to_all | solution.py:600
  21.7 8.4 %copy-start = (s32[1,64,16]{1,2,0:T(8,128)S(1)}, s32[1,64,16]{1,2,0:T(8,128)}, u32[]{:S(2)}) copy-start(s32[1,64,16]{1,2,0:T(8,128)} %param.16) | copy-start | bytes 12292
  21.7 8.3 %copy-start.1 = (s32[1,576]{1,0:T(1,128)S(1)}, s32[1,576]{1,0:T(1,128)}, u32[]{:S(2)}) copy-start(s32[1,576]{1,0:T(1,128)} %owned_ref.1) | copy-start | bytes 6916
  21.7 8.3 %copy-start.4 = (s32[1,64]{1,0:T(1,128)S(1)}, s32[1,64]{1,0:T(1,128)}, u32[]{:S(2)}) copy-start(s32[1,64]{1,0:T(1,128)} %length_ref.1) | copy-start | bytes 772
  45.6 17.4 %all-to-all-start.1 = ((bf16[64,16,256]{2,1,0:T(8,128)(2,1)}), bf16[64,16,256]{2,1,0:T(8,128)(2,1)S(1)}, u32[]{:S(2)}, u32[]{:S(2)}) async-start(bf16[64,16,256]{2,1,0:T(8,128)(2,1)} %bitcast.11), calls=%async_computation.1 | async-start | bytes 1048576 | tf_op jit(solution)/shard_map/all_to_all | solution.py:617
  52.1 10.8 %copy-start.2 = (f32[1,75,4]{1,2,0:T(4,128)S(1)}, f32[1,75,4]{1,2,0:T(4,128)}, u32[]{:S(2)}) copy-start(f32[1,75,4]{1,2,0:T(4,128)} %param.14) | copy-start | bytes 3604

commit v4 on v3

--- a/solution.py
+++ b/solution.py
@@ -10,9 +10,10 @@
 NSTEP = 16
 LANES = 128
 GROUP = 8
+MANY = 2
 WIDTH = 4096
 FIRST = 2
-SECOND = 4
+SECOND = 3
 BF16 = jnp.bfloat16
 F32 = jnp.float32
 
@@ -122,6 +123,19 @@
     )
 
 
+def fill_spread(spread):
+    row = lax.broadcasted_iota(jnp.int32, spread.shape, 0)
+    col = lax.broadcasted_iota(jnp.int32, spread.shape, 1)
+    source = (col >> 9) * BLK + ((col >> 3) & 31) * 2 + ((col >> 8) & 1)
+    spread[...] = jnp.where(row == source, 1.0, 0.0).astype(BF16)
+
+
+def own_slot(rows, cols):
+    row = lax.broadcasted_iota(jnp.int32, (rows, cols), 0)
+    col = lax.broadcasted_iota(jnp.int32, (rows, cols), 1)
+    return (row & 7) == (col & 7)
+
+
 def pick(values, lanes):
     return jnp.take_along_axis(values, lanes, axis=1, mode="promise_in_bounds")
 
@@ -181,6 +195,8 @@
     in_table_ref,
     swept_hbm,
     chosen,
+    spread,
+    wide,
     weights,
     state,
     coef,
@@ -257,28 +273,33 @@
 
     @pl.when(jnp.logical_not(first))
     def _():
-        own = (lane & 7) == row
+        fill_spread(spread)
         left = lane < BLK
+        mine = own_slot(MANY * LANES, 2 * LANES)
 
         def lists(part, carry):
-            fetch_weights(weights_hbm, weights, weight_sems, part).wait()
-            for inner in range(GROUP):
-                tile = part * GROUP + inner
+            span = MANY * LANES
+            here = pl.ds(pl.multiple_of(part * span, span), span)
+            for duo in range(NF // 2):
+                values = chosen[here, duo * LANES : (duo + 1) * LANES].astype(BF16)
+                for chunk in range(4):
+                    cols = slice(chunk * 2 * LANES, (chunk + 1) * 2 * LANES)
+                    spaced = jnp.dot(values, spread[:, cols], preferred_element_type=F32)
+                    wide[:, (duo * 4 + chunk) * 2 * LANES : (duo * 4 + chunk + 1) * 2 * LANES] = (
+                        jnp.where(mine, spaced, 0.0)
+                    )
+            for piece in range(MANY):
+                fetch_weights(weights_hbm, weights, weight_sems, part * MANY + piece).wait()
+            for inner in range(MANY * GROUP):
+                tile = part * MANY * GROUP + inner
                 rows = pl.ds(pl.multiple_of(tile * 16, 16), 16)
-                values = chosen[rows, :]
                 results = []
                 for half in range(2):
-                    lines = []
-                    for field in range(NF):
-                        duo = values[
-                            half * 8 : half * 8 + 8, field // 2 * LANES : (field // 2 + 1) * LANES
-                        ]
-                        for parity in range(2):
-                            line = []
-                            for side in range(2):
-                                source = (field % 2) * BLK + 2 * (side * 16 + (lane >> 3)) + parity
-                                line.append(jnp.where(own, pick(duo, source), 0.0))
-                            lines.append(jnp.concatenate(line, 1))
+                    start = inner * 16 + half * 8
+                    lines = [
+                        wide[start : start + 8, line * 2 * LANES : (line + 1) * 2 * LANES]
+                        for line in range(2 * NF)
+                    ]
                     product = jnp.dot(
                         jnp.concatenate(lines, 0).astype(BF16),
                         half_list(weights, tile, half),
@@ -299,14 +320,14 @@
                     ).astype(BF16)
             return carry
 
-        lax.fori_loop(0, parts, lists, 0)
+        lax.fori_loop(0, parts // MANY, lists, 0)
 
     for block in range(count):
         store(block).wait()
 
 
 def outgoing(section, atmos, length, ids, owned, blocks, ops, weights, state, coef, swept):
-    lists, halves, cap, square = weights.shape
+    lists, halves, cap, _ = weights.shape
     slots = lists * halves * cap
     count, width = blocks.shape
     padded = -(-count // LANES) * LANES
@@ -327,6 +348,8 @@
         input_output_aliases={10: 3},
         scratch_shapes=[
             pltpu.VMEM((slots, width), F32),
+            pltpu.VMEM((LANES, 8 * LANES), BF16),
+            pltpu.VMEM((MANY * LANES, 16 * LANES), F32),
             pltpu.VMEM(weights.shape, BF16),
             held,
             held,
@@ -344,7 +367,7 @@
 
 
 def early_sweep(ops, state, coef, swept, start, stop):
-    levels, cells = state.shape
+    levels, _ = state.shape
     columns = pl.BlockSpec((levels, WIDTH), lambda i: (0, early_column(i + start)))
     there = pl.BlockSpec(memory_space=pl.ANY)
     return pl.pallas_call(
@@ -359,20 +382,17 @@
     )(ops, state, coef, swept)
 
 
-def backward_lists(arrived_ref, weights_hbm, weights, terms, weight_sems):
-    lane = lax.broadcasted_iota(jnp.int32, (8, LANES), 1)
-    row = lax.broadcasted_iota(jnp.int32, (8, LANES), 0)
-    left = lane < BLK
-    source = (((lane >> 1) & 15) << 3) + row
-    half_kind = ((lane >> 5) & 1) * 2 + (lane & 1)
+def backward_lists(arrived_ref, weights_hbm, weights, terms, spread, wide, weight_sems):
+    left = lanes_below((8, LANES), BLK)
+    mine = own_slot(8, 2 * LANES)
+    fill_spread(spread)
 
     def lists(part, carry):
-        fetch_weights(weights_hbm, weights, weight_sems, part).wait()
-        for inner in range(GROUP):
-            tile = part * GROUP + inner
-            rows = pl.ds(pl.multiple_of(tile * 16, 16), 16)
-            echoes = arrived_ref[rows, :].astype(F32)
-            results = []
+        for piece in range(MANY):
+            fetch_weights(weights_hbm, weights, weight_sems, part * MANY + piece).wait()
+        for inner in range(MANY * GROUP):
+            tile = part * MANY * GROUP + inner
+            echoes = arrived_ref[pl.ds(pl.multiple_of(tile * 16, 16), 16), :].astype(F32)
             for half in range(2):
                 lines = []
                 for duo in range(NF // 2):
@@ -390,34 +410,23 @@
                     (((1,), (1,)), ((), ())),
                     preferred_element_type=F32,
                 )
-                outs = []
-                for duo in range(NF // 2):
-                    fields = []
-                    for field in (2 * duo, 2 * duo + 1):
-                        total = None
-                        for side in range(2):
-                            for parity in range(2):
-                                start = field * 16 + parity * 8
-                                value = pick(
-                                    product[start : start + 8, side * LANES : (side + 1) * LANES],
-                                    source,
-                                )
-                                kind = side * 2 + parity
-                                total = (
-                                    value
-                                    if total is None
-                                    else jnp.where(half_kind == kind, value, total)
-                                )
-                        fields.append(total)
-                    outs.append(jnp.where(left, fields[0], fields[1]))
-                results.append(outs)
-            for duo in range(NF // 2):
-                terms[rows, duo * LANES : (duo + 1) * LANES] = jnp.concatenate(
-                    [results[0][duo], results[1][duo]], 0
-                ).astype(BF16)
+                start = inner * 16 + half * 8
+                for line in range(2 * NF):
+                    wide[start : start + 8, line * 2 * LANES : (line + 1) * 2 * LANES] = jnp.where(
+                        mine, product[line * 8 : line * 8 + 8], 0.0
+                    )
+        span = MANY * LANES
+        here = pl.ds(pl.multiple_of(part * span, span), span)
+        for duo in range(NF // 2):
+            terms[here, duo * LANES : (duo + 1) * LANES] = lax.dot_general(
+                wide[:, duo * 8 * LANES : (duo + 1) * 8 * LANES].astype(BF16),
+                spread[...],
+                (((1,), (1,)), ((), ())),
+                preferred_element_type=F32,
+            ).astype(BF16)
         return carry
 
-    lax.fori_loop(0, weights.shape[0] // GROUP, lists, 0)
+    lax.fori_loop(0, weights.shape[0] // GROUP // MANY, lists, 0)
 
 
 def sum_terms(key_ref, table_ref, terms, forcing):
@@ -459,6 +468,8 @@
     forcing,
     early,
     last,
+    spread,
+    wide,
     weights,
     weight_sems,
     sems,
@@ -495,7 +506,7 @@
 
     @pl.when(backward)
     def _():
-        backward_lists(arrived_ref, weights_hbm, weights, terms, weight_sems)
+        backward_lists(arrived_ref, weights_hbm, weights, terms, spread, wide, weight_sems)
 
     @pl.when(step == 0)
     def _():
@@ -567,6 +578,8 @@
             pltpu.VMEM((cells // LANES * 8, LANES), F32),
             pltpu.VMEM((2, levels, 2 * WIDTH), BF16),
             pltpu.VMEM((2, levels, WIDTH), BF16),
+            pltpu.VMEM((LANES, 8 * LANES), BF16),
+            pltpu.VMEM((MANY * LANES, 16 * LANES), F32),
             pltpu.VMEM(weights.shape, BF16),
             pltpu.SemaphoreType.DMA((weights.shape[0] // GROUP,)),
             pltpu.SemaphoreType.DMA((4,)),
@@ -598,7 +611,8 @@
     ops = column_ops[0].transpose(0, 2, 1)
     which = section.reshape(1).astype(jnp.int32)
     arrived_ids = lax.all_to_all(pair_ocean[0], "tile", split_axis=0, concat_axis=0, tiled=True)
-    surface, swept = surface_blocks(surf_read[0], ops, state, coef)
+    read = pltpu.with_memory_space_constraint(surf_read[0], pltpu.HBM)
+    surface, swept = surface_blocks(read, ops, state, coef)
     partner = lax.ppermute(surface, "sec", [(0, 1), (1, 0)])
     swept = early_sweep(ops, state, coef, swept, 1, FIRST)
     payload, in_key, in_table, swept = outgoing(

time: 77.8 us -> 74.1 us (0.952)
  waiting for transfers between devices: 6.08 us -> 3.28 us
    pallas_call x1, Pallas kernels: 15.5 us -> 11.7 us  [outgoing(): pl.pallas_call(outgoing_kernel, out_shape=(jax.ShapeDtypeStruct((slots, w...]
    pallas_call x2, Pallas kernels: 13 us -> 15.9 us  [early_sweep(): pl.pallas_call(early_kernel, grid=(stop - start,), out_shape=pltpu.HBM(sw...]
    all_to_all x1, waiting for transfers between devices: 2.82 us -> 0.01 us  [body(): lax.all_to_all(payload.reshape(lists, cap, NF * BLK), 'tile', split_axis=...]
    unnamed x14 -> x12, local copies, waits for them, and re-layouts: 2.75 us -> 2.06 us
  transfers between devices with their start and end apart: 3 -> 3, of which waited for: 2 -> 1; matrix products, arithmetic and copies ran while one was open for 1% -> 1% of each run, Pallas kernels for 17% -> 22%
where the time goes in v4:
time: 74.1 us; the launch traced here: 73.7 us
  Pallas kernels  48.9 us (66%)
  starting transfers between devices  19.2 us (26%)
  waiting for transfers between devices  3.28 us (4%)
  local copies, waits for them, and re-layouts  2.06 us (3%)
    pallas_call x2, Pallas kernels, early_sweep(): pl.pallas_call(early_kernel, grid=(stop - start,), out_shape=pltpu.HBM(sw...  15.9 us
    pallas_call x1, Pallas kernels, late(): pl.pallas_call(late_kernel, grid=(cells // (3 * WIDTH),), out_shape=jax.S...  14.4 us
    pallas_call x1, Pallas kernels, outgoing(): pl.pallas_call(outgoing_kernel, out_shape=(jax.ShapeDtypeStruct((slots, w...  11.7 us
    all_to_all x1, starting transfers between devices, body(): lax.all_to_all(pair_ocean[0], 'tile', split_axis=0, concat_axis=0, tiled=...  11.2 us
    pallas_call x1, Pallas kernels, surface_blocks(): pl.pallas_call(surface_kernel, out_shape=(jax.ShapeDtypeStruct((blocks, N...  6.91 us
    all_to_all x1, starting transfers between devices, body(): lax.all_to_all(payload.reshape(lists, cap, NF * BLK), 'tile', split_axis=...  6.52 us
    all_to_all x1, waiting for transfers between devices, body(): lax.all_to_all(pair_ocean[0], 'tile', split_axis=0, concat_axis=0, tiled=...  3.27 us
    unnamed x12, local copies, waits for them, and re-layouts  2.06 us
  transfers between devices with their start and end apart: 3, of which 1 were waited for; matrix products, arithmetic and copies ran while one was open for 1% of the time, Pallas kernels for 22%

profile of v4, /device:TPU:1, one launch (start us, length us, event | category | flops | bytes accessed | tf_op | source)
XLA Modules:
  0.0 73.7 jit_solution(4973739304147182008)
XLA Ops:
  0.0 1.3 %copy.15 = bf16[1,16,75,75]{2,3,1,0:T(8,128)(2,1)S(1)} copy(bf16[1,16,75,75]{3,1,2,0:T(8,128)(2,1)} %param.12) | data formatting | bytes 360000 | tf_op args[2]
  1.3 0.0 copy-start.4
  1.3 6.9 %surface.1 = (bf16[576,256]{1,0:T(8,128)(2,1)S(1)}, bf16[75,24576]{1,0:T(8,128)(2,1)}) custom-call(bf16[4,75]{1,0:T(4,128)(2,1)} %bitcast.38, bf16[16,75,75]{2,1,0:T(8,128)(2,1)S(1)} %bitcast.18, bf16[75,36864]{1,0:T(8,128)(2,1)} %bitcast.26, bf16[75,36864]{1,0:T(8,128)(2,1)} %bitcast.31), custom_call_target="tpu_custom_call" | custom-call | tf_op jit(solution)/shard_map/surface/pallas_call | solution.py:95
  8.3 1.5 %collective-permute-start = (bf16[576,256]{1,0:T(8,128)(2,1)S(1)}, bf16[576,256]{1,0:T(8,128)(2,1)S(1)}, u32[]{:S(2)}, u32[]{:S(2)}) collective-permute-start(bf16[576,256]{1,0:T(8,128)(2,1)S(1)} %get-tuple-element.11), channel_id=1, source_target_pairs={{0,64},{64,0},{1,65},{65,1},{2,66},{66,2},{3,67},{67,3},{4,68},{68... | collective-permute-start | bytes 884744 | tf_op jit(solution)/shard_map/ppermute | solution.py:616
  9.7 0.0 copy-done.4
  9.7 0.7 copy.14
  10.4 11.2 %all-to-all-start = ((s32[64,1,16]{2,1,0:T(1,128)}), s32[64,1,16]{2,1,0:T(1,128)S(1)}, u32[]{:S(2)}, u32[]{:S(2)}) async-start(s32[64,1,16]{2,1,0:T(1,128)} %bitcast.3), calls=%async_computation | async-start | bytes 65536 | tf_op jit(solution)/shard_map/all_to_all | solution.py:613
  21.7 0.0 copy-start
  21.7 0.0 copy-start.1
  21.7 0.0 copy-start.3
  21.7 5.0 %early.2.swept_in = bf16[75,24576]{1,0:T(8,128)(2,1)} custom-call(bf16[16,75,75]{2,1,0:T(8,128)(2,1)S(1)} %bitcast.19, bf16[75,36864]{1,0:T(8,128)(2,1)} %bitcast.27, bf16[75,36864]{1,0:T(8,128)(2,1)} %bitcast.32, bf16[75,24576]{1,0:T(8,128)(2,1)} %get-tuple-element.12.swept_hbm), custom_call_target="tpu_custom_call", output_to_operand_aliasing={{}: (3, {})} | custom-call | tf_op jit(solution)/shard_map/early/pallas_call | solution.py:373
  26.8 3.3 %all-to-all-done.ids_ref = s32[64,1,16]{2,1,0:T(1,128)S(1)} async-done(((s32[64,1,16]{2,1,0:T(1,128)}), s32[64,1,16]{2,1,0:T(1,128)S(1)}, u32[]{:S(2)}, u32[]{:S(2)}) %all-to-all-start) | async-done | bytes 4128 | tf_op jit(solution)/shard_map/all_to_all | solution.py:613
  30.0 0.0 collective-permute-done.blocks_ref
  30.0 0.0 copy-done
  30.0 0.0 copy-done.1
  30.0 0.0 copy-done.3
  30.1 11.7 %outgoing.1 = (bf16[1024,256]{1,0:T(8,128)(2,1)}, f32[8,128]{1,0:T(8,128)S(1)}, f32[1,640]{1,0:T(1,128)S(1)}, bf16[75,24576]{1,0:T(8,128)(2,1)}) custom-call(s32[1]{0:T(128)} %bitcast.section_ref, s32[16,64]{1,0:T(8,128)S(1)} %bitcast.24, s32[1,64]{1,0:T(1,128)S(1)} %copy-done.3, ...), custom_call_target="tpu_custom_call", output_to_operand_aliasing={{3}: (10, {})} | custom-call | tf_op jit(solution)/shard_map/outgoing/pallas_call | solution.py:338
  41.7 6.5 %all-to-all-start.1 = ((bf16[64,16,256]{2,1,0:T(8,128)(2,1)}), bf16[64,16,256]{2,1,0:T(8,128)(2,1)S(1)}, u32[]{:S(2)}, u32[]{:S(2)}) async-start(bf16[64,16,256]{2,1,0:T(8,128)(2,1)} %bitcast.11), calls=%async_computation.1 | async-start | bytes 1048576 | tf_op jit(solution)/shard_map/all_to_all | solution.py:631
  48.3 0.0 copy-start.2
  48.3 10.9 %early.3.swept_ref = bf16[75,24576]{1,0:T(8,128)(2,1)} custom-call(bf16[16,75,75]{2,1,0:T(8,128)(2,1)S(1)} %bitcast.21, bf16[75,36864]{1,0:T(8,128)(2,1)} %bitcast.29, bf16[75,36864]{1,0:T(8,128)(2,1)} %bitcast.34, bf16[75,24576]{1,0:T(8,128)(2,1)} %get-tuple-element.16.swept_hbm), custom_call_target="tpu_custom_call", output_to_operand_aliasing={{}: (3, {})} | custom-call | tf_op jit(solution)/shard_map/early/pallas_call | solution.py:373
  59.1 0.0 all-to-all-done.1
  59.2 0.0 copy-done.2
  59.2 14.4 %late.1 = bf16[75,36864]{1,0:T(8,128)(2,1)} custom-call(s32[1]{0:T(128)} %bitcast.section_ref, f32[8,128]{1,0:T(8,128)S(1)} %get-tuple-element.13.key_ref, f32[1,640]{1,0:T(1,128)S(1)} %get-tuple-element.14.table_ref, bf16[1024,256]{1,0:T(8,128)(2,1)S(1)} %bitcast.23, bf16[64,2,8,4096]{3,2,1,0:T(8,128)(2,1)} %bitcast.37, f32[4,75]{1,0:T(4,128)S(1)} %bitcast.25, ...), custom_call_target="tpu_custom_call" | custom-call | tf_op jit(solution)/shard_map/late/pallas_call | solution.py:559
Async XLA Ops:
  1.3 8.4 %copy-start.4 = (s32[1,64,16]{1,2,0:T(8,128)S(1)}, s32[1,64,16]{1,2,0:T(8,128)}, u32[]{:S(2)}) copy-start(s32[1,64,16]{1,2,0:T(8,128)} %param.17) | copy-start | bytes 12292
  8.3 21.8 %collective-permute-start = (bf16[576,256]{1,0:T(8,128)(2,1)S(1)}, bf16[576,256]{1,0:T(8,128)(2,1)S(1)}, u32[]{:S(2)}, u32[]{:S(2)}) collective-permute-start(bf16[576,256]{1,0:T(8,128)(2,1)S(1)} %get-tuple-element.11), channel_id=1, source_target_pairs={{0,64},{64,0},{1,65},{65,1},{2,66},{66,2},{3,67},{67,3},{4,68},{68... | collective-permute-start | bytes 884744 | tf_op jit(solution)/shard_map/ppermute | solution.py:616
  10.4 19.6 %all-to-all-start = ((s32[64,1,16]{2,1,0:T(1,128)}), s32[64,1,16]{2,1,0:T(1,128)S(1)}, u32[]{:S(2)}, u32[]{:S(2)}) async-start(s32[64,1,16]{2,1,0:T(1,128)} %bitcast.3), calls=%async_computation | async-start | bytes 65536 | tf_op jit(solution)/shard_map/all_to_all | solution.py:613
  21.7 8.4 %copy-start = (s32[1,64,16]{1,2,0:T(8,128)S(1)}, s32[1,64,16]{1,2,0:T(8,128)}, u32[]{:S(2)}) copy-start(s32[1,64,16]{1,2,0:T(8,128)} %param.16) | copy-start | bytes 12292
  21.7 8.3 %copy-start.1 = (s32[1,576]{1,0:T(1,128)S(1)}, s32[1,576]{1,0:T(1,128)}, u32[]{:S(2)}) copy-start(s32[1,576]{1,0:T(1,128)} %owned_ref.1) | copy-start | bytes 6916
  21.7 8.3 %copy-start.3 = (s32[1,64]{1,0:T(1,128)S(1)}, s32[1,64]{1,0:T(1,128)}, u32[]{:S(2)}) copy-start(s32[1,64]{1,0:T(1,128)} %length_ref.1) | copy-start | bytes 772
  41.7 17.4 %all-to-all-start.1 = ((bf16[64,16,256]{2,1,0:T(8,128)(2,1)}), bf16[64,16,256]{2,1,0:T(8,128)(2,1)S(1)}, u32[]{:S(2)}, u32[]{:S(2)}) async-start(bf16[64,16,256]{2,1,0:T(8,128)(2,1)} %bitcast.11), calls=%async_computation.1 | async-start | bytes 1048576 | tf_op jit(solution)/shard_map/all_to_all | solution.py:631
  48.3 10.9 %copy-start.2 = (f32[1,75,4]{1,2,0:T(4,128)S(1)}, f32[1,75,4]{1,2,0:T(4,128)}, u32[]{:S(2)}) copy-start(f32[1,75,4]{1,2,0:T(4,128)} %param.14) | copy-start | bytes 3604

commit v5 on v4

--- a/solution.py
+++ b/solution.py
@@ -12,7 +12,7 @@
 GROUP = 8
 MANY = 2
 WIDTH = 4096
-FIRST = 2
+FIRST = 1
 SECOND = 3
 BF16 = jnp.bfloat16
 F32 = jnp.float32
@@ -25,7 +25,9 @@
 def advance(ops_ref, current, coef):
     factors = coef.astype(F32)
     for step in range(NSTEP):
-        stepped = jnp.dot(ops_ref[step], current, preferred_element_type=F32)
+        stepped = lax.dot_general(
+            ops_ref[step], current, (((0,), (0,)), ((), ())), preferred_element_type=F32
+        )
         current = (stepped * factors).astype(BF16)
     return current
 
@@ -456,14 +458,15 @@
     section_ref,
     key_ref,
     table_ref,
-    arrived_ref,
+    arrived_hbm,
     weights_hbm,
     write_ref,
     ops_ref,
-    swept_ref,
+    swept_hbm,
     state_ref,
     coef_ref,
     out_hbm,
+    arrived,
     terms,
     forcing,
     early,
@@ -476,13 +479,24 @@
 ):
     step = pl.program_id(0)
     backward = jnp.logical_and(step == 0, section_ref[0] == 0)
+    slot = step % 2
+    before = 1 - slot
+    arrival = pltpu.make_async_copy(arrived_hbm, arrived, sems.at[6])
+
+    def fetch(block, into):
+        columns = pl.ds(pl.multiple_of(block * 2 * WIDTH, 2 * WIDTH), 2 * WIDTH)
+        return pltpu.make_async_copy(swept_hbm.at[:, columns], early.at[into], sems.at[4 + into])
+
+    @pl.when(step == 0)
+    def _():
+        arrival.start()
+        fetch(step, slot).start()
 
     @pl.when(backward)
     def _():
         for part in range(weight_sems.shape[0]):
             fetch_weights(weights_hbm, weights, weight_sems, part).start()
 
-    slot = step % 2
     span = 3 * WIDTH
     ready = pltpu.make_async_copy(
         early.at[slot],
@@ -494,7 +508,6 @@
         out_hbm.at[:, pl.ds(pl.multiple_of(step * span + 2 * WIDTH, WIDTH), WIDTH)],
         sems.at[2 + slot],
     )
-    before = 1 - slot
     ready_before = pltpu.make_async_copy(
         early.at[before], out_hbm.at[:, pl.ds(0, 2 * WIDTH)], sems.at[before]
     )
@@ -506,13 +519,15 @@
 
     @pl.when(backward)
     def _():
-        backward_lists(arrived_ref, weights_hbm, weights, terms, spread, wide, weight_sems)
+        arrival.wait()
+        backward_lists(arrived, weights_hbm, weights, terms, spread, wide, weight_sems)
 
     @pl.when(step == 0)
     def _():
         @pl.when(section_ref[0] == 1)
         def _():
-            terms[...] = arrived_ref[...]
+            arrival.wait()
+            terms[...] = arrived[...]
 
         sum_terms(key_ref, table_ref, terms, forcing)
 
@@ -535,7 +550,8 @@
             factor, operand, (((0,), (0,)), ((), ())), preferred_element_type=F32
         )
 
-    early[slot] = (swept_ref[...].astype(F32) + added(0, 2 * WIDTH)).astype(BF16)
+    fetch(step, slot).wait()
+    early[slot] = (early[slot].astype(F32) + added(0, 2 * WIDTH)).astype(BF16)
     ready.start()
     last[slot] = (last[slot].astype(F32) + added(2 * WIDTH, WIDTH)).astype(BF16)
     swept.start()
@@ -544,6 +560,10 @@
     def _():
         ready_before.wait()
         swept_before.wait()
+
+    @pl.when(step < pl.num_programs(0) - 1)
+    def _():
+        fetch(step + 1, before).start()
 
     @pl.when(step == pl.num_programs(0) - 1)
     def _():
@@ -564,16 +584,17 @@
             pl.BlockSpec(memory_space=pltpu.SMEM),
             whole,
             whole,
-            whole,
+            pl.BlockSpec(memory_space=pl.ANY),
             pl.BlockSpec(memory_space=pl.ANY),
             whole,
             whole,
-            pl.BlockSpec((levels, 2 * WIDTH), lambda i: (0, i)),
+            pl.BlockSpec(memory_space=pl.ANY),
             columns,
             columns,
         ],
         out_specs=pl.BlockSpec(memory_space=pl.ANY),
         scratch_shapes=[
+            pltpu.VMEM((slots, width), BF16),
             pltpu.VMEM((slots, width), BF16),
             pltpu.VMEM((cells // LANES * 8, LANES), F32),
             pltpu.VMEM((2, levels, 2 * WIDTH), BF16),
@@ -582,7 +603,7 @@
             pltpu.VMEM((MANY * LANES, 16 * LANES), F32),
             pltpu.VMEM(weights.shape, BF16),
             pltpu.SemaphoreType.DMA((weights.shape[0] // GROUP,)),
-            pltpu.SemaphoreType.DMA((4,)),
+            pltpu.SemaphoreType.DMA((7,)),
         ],
         compiler_params=pltpu.CompilerParams(vmem_limit_bytes=36 << 20),
         name="late",
@@ -608,13 +629,12 @@
     weights = pltpu.with_memory_space_constraint(
         remap_weights[0].reshape(lists, cap // 8, 8, BLK * BLK), pltpu.HBM
     )
-    ops = column_ops[0].transpose(0, 2, 1)
+    ops = column_ops[0]
     which = section.reshape(1).astype(jnp.int32)
     arrived_ids = lax.all_to_all(pair_ocean[0], "tile", split_axis=0, concat_axis=0, tiled=True)
     read = pltpu.with_memory_space_constraint(surf_read[0], pltpu.HBM)
     surface, swept = surface_blocks(read, ops, state, coef)
     partner = lax.ppermute(surface, "sec", [(0, 1), (1, 0)])
-    swept = early_sweep(ops, state, coef, swept, 1, FIRST)
     payload, in_key, in_table, swept = outgoing(
         which,
         pair_atmos[0].T,

time: 74.1 us -> 75.6 us (1.020); the launches traced: 73.7 us -> 74.4 us
  waiting for transfers between devices: 3.28 us -> 8.35 us
  Pallas kernels: 48.9 us -> 46.5 us
  starting transfers between devices: 19.2 us -> 17.6 us
    all_to_all x1, waiting for transfers between devices: 3.27 us -> 8.35 us  [body(): lax.all_to_all(pair_ocean[0], 'tile', split_axis=0, concat_axis=0, tiled=...]
    pallas_call x2 -> x1, Pallas kernels: 15.9 us -> 11 us  [early_sweep(): pl.pallas_call(early_kernel, grid=(stop - start,), out_shape=pltpu.HBM(sw...]
    pallas_call x1, Pallas kernels: 11.7 us -> 14.3 us  [outgoing(): pl.pallas_call(outgoing_kernel, out_shape=(jax.ShapeDtypeStruct((slots, w...]
    all_to_all x1, starting transfers between devices: 6.52 us -> 4.87 us  [body(): lax.all_to_all(payload.reshape(lists, cap, NF * BLK), 'tile', split_axis=...]
  transfers between devices with their start and end apart: 3 -> 3, of which waited for: 1 -> 1; matrix products, arithmetic and copies ran while one was open for 1% -> 1% of each run, Pallas kernels for 22% -> 15%
where the time goes in v5:
time: 75.6 us; the launch traced here: 74.4 us
  Pallas kernels  46.5 us (62%)
  starting transfers between devices  17.6 us (23%)
  waiting for transfers between devices  8.35 us (11%)
  local copies, waits for them, and re-layouts  1.78 us (2%)
    pallas_call x1, Pallas kernels, outgoing(): pl.pallas_call(outgoing_kernel, out_shape=(jax.ShapeDtypeStruct((slots, w...  14.3 us
    pallas_call x1, Pallas kernels, late(): pl.pallas_call(late_kernel, grid=(cells // (3 * WIDTH),), out_shape=jax.S...  14.2 us
    all_to_all x1, starting transfers between devices, body(): lax.all_to_all(pair_ocean[0], 'tile', split_axis=0, concat_axis=0, tiled=...  11.2 us
    pallas_call x1, Pallas kernels, early_sweep(): pl.pallas_call(early_kernel, grid=(stop - start,), out_shape=pltpu.HBM(sw...  11 us
    all_to_all x1, waiting for transfers between devices, body(): lax.all_to_all(pair_ocean[0], 'tile', split_axis=0, concat_axis=0, tiled=...  8.35 us
    pallas_call x1, Pallas kernels, surface_blocks(): pl.pallas_call(surface_kernel, out_shape=(jax.ShapeDtypeStruct((blocks, N...  6.97 us
    all_to_all x1, starting transfers between devices, body(): lax.all_to_all(payload.reshape(lists, cap, NF * BLK), 'tile', split_axis=...  4.87 us
    unnamed x12, local copies, waits for them, and re-layouts  1.78 us
  transfers between devices with their start and end apart: 3, of which 1 were waited for; matrix products, arithmetic and copies ran while one was open for 1% of the time, Pallas kernels for 15%

profile of v5, /device:TPU:1, one launch (start us, length us, event | category | flops | bytes accessed | tf_op | source)
XLA Modules:
  0.0 74.4 jit_solution(7738837132458112826)
XLA Ops:
  0.0 1.0 %copy.16 = bf16[1,16,75,75]{3,2,1,0:T(8,128)(2,1)S(1)} copy(bf16[1,16,75,75]{3,1,2,0:T(8,128)(2,1)} %param.12) | data formatting | bytes 360000 | tf_op args[2]
  1.1 0.0 copy-start.4
  1.1 0.0 copy-start
  1.1 0.0 copy-start.1
  1.1 0.0 copy-start.3
  1.1 7.0 %surface.1 = (bf16[576,256]{1,0:T(8,128)(2,1)S(1)}, bf16[75,24576]{1,0:T(8,128)(2,1)}) custom-call(bf16[4,75]{1,0:T(4,128)(2,1)} %bitcast.35, bf16[16,75,75]{2,1,0:T(8,128)(2,1)S(1)} %bitcast.18, bf16[75,36864]{1,0:T(8,128)(2,1)} %bitcast.25, bf16[75,36864]{1,0:T(8,128)(2,1)} %bitcast.29), custom_call_target="tpu_custom_call" | custom-call | tf_op jit(solution)/shard_map/surface/pallas_call | solution.py:97
  8.1 1.5 %collective-permute-start = (bf16[576,256]{1,0:T(8,128)(2,1)S(1)}, bf16[576,256]{1,0:T(8,128)(2,1)S(1)}, u32[]{:S(2)}, u32[]{:S(2)}) collective-permute-start(bf16[576,256]{1,0:T(8,128)(2,1)S(1)} %get-tuple-element.11), channel_id=1, source_target_pairs={{0,64},{64,0},{1,65},{65,1},{2,66},{66,2},{3,67},{67,3},{4,68},{68... | collective-permute-start | bytes 884744 | tf_op jit(solution)/shard_map/ppermute | solution.py:637
  9.5 0.0 copy-done.4
  9.5 0.7 copy.13
  10.2 11.2 %all-to-all-start = ((s32[64,1,16]{2,1,0:T(1,128)}), s32[64,1,16]{2,1,0:T(1,128)S(1)}, u32[]{:S(2)}, u32[]{:S(2)}) async-start(s32[64,1,16]{2,1,0:T(1,128)} %bitcast.3), calls=%async_computation | async-start | bytes 65536 | tf_op jit(solution)/shard_map/all_to_all | solution.py:634
  21.5 8.3 %all-to-all-done.ids_ref = s32[64,1,16]{2,1,0:T(1,128)S(1)} async-done(((s32[64,1,16]{2,1,0:T(1,128)}), s32[64,1,16]{2,1,0:T(1,128)S(1)}, u32[]{:S(2)}, u32[]{:S(2)}) %all-to-all-start) | async-done | bytes 4128 | tf_op jit(solution)/shard_map/all_to_all | solution.py:634
  29.8 0.0 collective-permute-done.blocks_ref
  29.8 0.0 copy-done
  29.8 0.0 copy-done.1
  29.8 0.0 copy-done.3
  29.9 14.3 %outgoing.1 = (bf16[1024,256]{1,0:T(8,128)(2,1)}, f32[8,128]{1,0:T(8,128)S(1)}, f32[1,640]{1,0:T(1,128)S(1)}, bf16[75,24576]{1,0:T(8,128)(2,1)}) custom-call(s32[1]{0:T(128)} %bitcast.section_ref, s32[16,64]{1,0:T(8,128)S(1)} %bitcast.23, s32[1,64]{1,0:T(1,128)S(1)} %copy-done.3, ...), custom_call_target="tpu_custom_call", output_to_operand_aliasing={{3}: (10, {})} | custom-call | tf_op jit(solution)/shard_map/outgoing/pallas_call | solution.py:340
  44.2 4.9 %all-to-all-start.1 = ((bf16[64,16,256]{2,1,0:T(8,128)(2,1)}), bf16[64,16,256]{2,1,0:T(8,128)(2,1)S(1)}, u32[]{:S(2)}, u32[]{:S(2)}) async-start(bf16[64,16,256]{2,1,0:T(8,128)(2,1)} %bitcast.9), calls=%async_computation.1 | async-start | bytes 1048576 | tf_op jit(solution)/shard_map/all_to_all | solution.py:651
  49.0 0.0 copy-start.2
  49.1 11.0 %early.1.swept_hbm = bf16[75,24576]{1,0:T(8,128)(2,1)} custom-call(bf16[16,75,75]{2,1,0:T(8,128)(2,1)S(1)} %bitcast.20, bf16[75,36864]{1,0:T(8,128)(2,1)} %bitcast.27, bf16[75,36864]{1,0:T(8,128)(2,1)} %bitcast.31, bf16[75,24576]{1,0:T(8,128)(2,1)} %get-tuple-element.16.swept_hbm), custom_call_target="tpu_custom_call", output_to_operand_aliasing={{}: (3, {})} | custom-call | tf_op jit(solution)/shard_map/early/pallas_call | solution.py:375
  60.1 0.0 all-to-all-done.1
  60.1 0.0 copy-done.2
  60.1 14.2 %late.1 = bf16[75,36864]{1,0:T(8,128)(2,1)} custom-call(s32[1]{0:T(128)} %bitcast.section_ref, f32[8,128]{1,0:T(8,128)S(1)} %get-tuple-element.13.key_ref, f32[1,640]{1,0:T(1,128)S(1)} %get-tuple-element.14.table_ref, bf16[1024,256]{1,0:T(8,128)(2,1)S(1)} %bitcast.22, bf16[64,2,8,4096]{3,2,1,0:T(8,128)(2,1)} %bitcast.34, f32[4,75]{1,0:T(4,128)S(1)} %bitcast.24, ...), custom_call_target="tpu_custom_call" | custom-call | tf_op jit(solution)/shard_map/late/pallas_call | solution.py:579
Async XLA Ops:
  1.1 8.5 %copy-start.4 = (s32[1,64,16]{1,2,0:T(8,128)S(1)}, s32[1,64,16]{1,2,0:T(8,128)}, u32[]{:S(2)}) copy-start(s32[1,64,16]{1,2,0:T(8,128)} %param.17) | copy-start | bytes 12292
  1.1 28.8 %copy-start = (s32[1,64,16]{1,2,0:T(8,128)S(1)}, s32[1,64,16]{1,2,0:T(8,128)}, u32[]{:S(2)}) copy-start(s32[1,64,16]{1,2,0:T(8,128)} %param.16) | copy-start | bytes 12292
  1.1 28.8 %copy-start.1 = (s32[1,576]{1,0:T(1,128)S(1)}, s32[1,576]{1,0:T(1,128)}, u32[]{:S(2)}) copy-start(s32[1,576]{1,0:T(1,128)} %owned_ref.1) | copy-start | bytes 6916
  1.1 28.8 %copy-start.3 = (s32[1,64]{1,0:T(1,128)S(1)}, s32[1,64]{1,0:T(1,128)}, u32[]{:S(2)}) copy-start(s32[1,64]{1,0:T(1,128)} %length_ref.1) | copy-start | bytes 772
  8.1 21.8 %collective-permute-start = (bf16[576,256]{1,0:T(8,128)(2,1)S(1)}, bf16[576,256]{1,0:T(8,128)(2,1)S(1)}, u32[]{:S(2)}, u32[]{:S(2)}) collective-permute-start(bf16[576,256]{1,0:T(8,128)(2,1)S(1)} %get-tuple-element.11), channel_id=1, source_target_pairs={{0,64},{64,0},{1,65},{65,1},{2,66},{66,2},{3,67},{67,3},{4,68},{68... | collective-permute-start | bytes 884744 | tf_op jit(solution)/shard_map/ppermute | solution.py:637
  10.2 19.6 %all-to-all-start = ((s32[64,1,16]{2,1,0:T(1,128)}), s32[64,1,16]{2,1,0:T(1,128)S(1)}, u32[]{:S(2)}, u32[]{:S(2)}) async-start(s32[64,1,16]{2,1,0:T(1,128)} %bitcast.3), calls=%async_computation | async-start | bytes 65536 | tf_op jit(solution)/shard_map/all_to_all | solution.py:634
  44.2 15.9 %all-to-all-start.1 = ((bf16[64,16,256]{2,1,0:T(8,128)(2,1)}), bf16[64,16,256]{2,1,0:T(8,128)(2,1)S(1)}, u32[]{:S(2)}, u32[]{:S(2)}) async-start(bf16[64,16,256]{2,1,0:T(8,128)(2,1)} %bitcast.9), calls=%async_computation.1 | async-start | bytes 1048576 | tf_op jit(solution)/shard_map/all_to_all | solution.py:651
  49.0 11.0 %copy-start.2 = (f32[1,75,4]{1,2,0:T(4,128)S(1)}, f32[1,75,4]{1,2,0:T(4,128)}, u32[]{:S(2)}) copy-start(f32[1,75,4]{1,2,0:T(4,128)} %param.14) | copy-start | bytes 3604
